TPU v7x, 256 devices: a whole 4x4x8 slice. The times are simulated.
256 devices in a mesh: term: 4 (over x), sector: 64 (over y, z, core).
Axes of the slice: x: 4, y: 4, z: 8, core: 2. Of those that a mesh axis runs over, the one named last changes fastest.
Arguments:
- psi_blocks: bfloat16 [4096, 128, 128], P('sector'), may hold values from -6 to 6
- right_ops: bfloat16 [8, 4096, 128, 128], P('term', 'sector'), may hold values from -0.5 to 0.5
- left_ops: bfloat16 [8, 4096, 128, 128], P('term', 'sector'), may hold values from -0.1875 to 0.1875
- owner_map: int32 [4096, 1], P('sector'), may hold values from 0 to 63; in each aligned block of 64 rows (0 to 63, 64 to 127, ...) at most 2 rows name the same one
- left_local: int32 [4096, 1], P('sector'), may hold values from 0 to 63
Outputs:
- sigma: bfloat16 [4096, 128, 128], P('sector', 'term')
Inputs may be any that keep to these rules, and one draw needn't show every extreme that they name: `owner_map`: among the 64 sectors held by one device along `sector` (aligned blocks), at most 2 name the same owner; some block reaches it.
All inputs are finite; a program needn't handle non-finite values.
Results may differ from a plain program's by a relative error of at most 0.0049.
Values may be sent and summed in bfloat16 or wider, within the bound.
A program may use at most 128 MiB of HBM per device.

v0:
```python
import jax
import jax.numpy as jnp
from jax import lax
from jax.sharding import PartitionSpec as P


def ranks_of(owners):
    count = owners.shape[-1]
    same = owners[..., :, None] == owners[..., None, :]
    earlier = lax.broadcasted_iota(jnp.int32, (count, count), 0) < lax.broadcasted_iota(
        jnp.int32, (count, count), 1
    )
    return jnp.sum((same & earlier).astype(jnp.int32), axis=-2)


def local(psi_blocks, right_ops, left_ops, owner_map, left_local):
    sec_dev = psi_blocks.shape[0]
    width = psi_blocks.shape[1]
    terms_dev = right_ops.shape[0]
    n_sector = lax.axis_size("sector")
    capacity = max(2, 2 * sec_dev // n_sector)
    slots = n_sector * capacity
    owners = owner_map[:, 0]
    slot_id = owners * capacity + ranks_of(owners)
    packer = (lax.broadcasted_iota(jnp.int32, (slots, sec_dev), 0) == slot_id[None, :]).astype(
        jnp.bfloat16
    )
    routes_all = lax.all_gather(
        jnp.concatenate([owner_map, left_local], axis=1), "sector", axis=0, tiled=True
    )
    all_owners = routes_all[:, 0].reshape(n_sector, sec_dev)
    all_local = routes_all[:, 1].reshape(n_sector, sec_dev)
    all_ranks = ranks_of(all_owners)
    mine = lax.axis_index("sector")
    slot_iota = lax.broadcasted_iota(jnp.int32, (1, 1, capacity), 2)
    hits = (all_owners == mine)[:, :, None] & (all_ranks[:, :, None] == slot_iota)
    tags = (jnp.sum(jnp.where(hits, all_local[:, :, None] + 1, 0), axis=1) - 1).reshape(slots)
    inter = jnp.einsum(
        "sij,tsjk->stik", psi_blocks, right_ops, preferred_element_type=jnp.float32
    ).astype(jnp.bfloat16)
    packed = jnp.dot(packer, inter.reshape(sec_dev, -1), preferred_element_type=jnp.float32).astype(
        jnp.bfloat16
    )
    arrived = lax.all_to_all(
        packed.reshape(n_sector, capacity, -1), "sector", split_axis=0, concat_axis=0, tiled=True
    )
    arrived = arrived.reshape(slots, terms_dev, width, width)
    picked = jnp.take(left_ops, jnp.clip(tags, 0, sec_dev - 1), axis=1)
    images = jnp.einsum("tnij,ntjk->nik", picked, arrived, preferred_element_type=jnp.float32)
    collect = (lax.broadcasted_iota(jnp.int32, (sec_dev, slots), 0) == tags[None, :]).astype(
        jnp.float32
    )
    partial_sum = jnp.dot(
        collect,
        images.reshape(slots, -1),
        precision=lax.Precision.HIGHEST,
        preferred_element_type=jnp.float32,
    ).reshape(sec_dev, width, width)
    total = lax.psum(partial_sum, "term")
    row_count = width // lax.axis_size("term")
    mine_rows = lax.dynamic_slice_in_dim(total, lax.axis_index("term") * row_count, row_count, 1)
    return mine_rows.astype(jnp.bfloat16)


def solution(mesh):
    placed = (
        P("sector", None, None),
        P("term", "sector", None, None),
        P("term", "sector", None, None),
        P("sector", None),
        P("sector", None),
    )
    return jax.shard_map(
        local, mesh=mesh, in_specs=placed, out_specs=P("sector", "term", None), check_vma=False
    )
```

profile of v0, /device:TPU:1, one launch (start us, length us, event | category | flops | bytes accessed | tf_op | source)
XLA Modules:
  0.0 411.3 jit_solution(9655905848802338681)
XLA Ops:
  0.0 0.0 copy-start
  0.0 0.9 convert_reduce_fusion.1
  0.9 0.7 multiply_add_fusion
  1.6 0.0 copy-done
  1.6 5.4 %convert_bitcast_fusion = bf16[64,2,128,128]{2,3,1,0:T(8,128)(2,1)} fusion(bf16[2,64,128,128]{3,2,1,0:T(8,128)(2,1)} %param.6, bf16[64,128,128]{2,1,0:T(8,128)(2,1)S(1)} %copy-done), kind=kOutput, calls=%fused_computation.12 | convolution fusion | flops 538968064 | bytes 10485760 | tf_op jit(solution)/shard_map/sij,tsjk->stik/dot_general | solution.py:38
  7.0 6.3 %copy.23 = bf16[64,2,128,128]{3,2,1,0:T(8,128)(2,1)} copy(bf16[64,2,128,128]{2,3,1,0:T(8,128)(2,1)} %convert_bitcast_fusion) | data formatting | bytes 8388608 | tf_op jit(solution)/shard_map/convert_element_type | solution.py:40
  13.4 8.8 %convolution_convert_fusion = bf16[128,32768]{1,0:T(8,128)(2,1)} fusion(bf16[8,8,256,128]{3,2,1,0:T(8,128)(2,1)} %bitcast.41, s32[64]{0:T(128)S(1)} %multiply_add_fusion), kind=kOutput, calls=%fused_computation.1 | convolution fusion | flops 541073408 | bytes 12583168 | tf_op jit(solution)/shard_map/dot_general | solution.py:41
  22.1 14.1 %reshape.90 = bf16[64,2,32768]{2,1,0:T(2,128)(2,1)} reshape(bf16[128,32768]{1,0:T(8,128)(2,1)} %convolution_convert_fusion) | data formatting | bytes 16777216 | tf_op jit(solution)/shard_map/reshape | solution.py:45
  36.3 0.0 copy-start.2
  36.3 0.0 copy-start.3
  36.3 13.5 %all-to-all-start = ((bf16[64,2,32768]{2,1,0:T(2,128)(2,1)}), bf16[64,2,32768]{2,1,0:T(2,128)(2,1)}, u32[]{:S(2)}, u32[]{:S(2)}) async-start(bf16[64,2,32768]{2,1,0:T(2,128)(2,1)} %reshape.90), calls=%async_computation | async-start | bytes 16777216 | tf_op jit(solution)/shard_map/all_to_all | solution.py:44
  49.8 0.0 copy-done.2
  49.8 0.0 copy-done.3
  49.8 218.2 %all-gather = s32[64,64,2]{1,2,0:T(2,128)S(1)} all-gather(s32[1,64,2]{1,2,0:T(2,128)S(1)} %add_bitcast_fusion), channel_id=1, replica_groups=mesh['term'=4,'sector'=64] {'sector'}, dimensions={0}, use_global_device_ids=true | all-gather | bytes 33280 | tf_op jit(solution)/shard_map/all_gather | solution.py:28
  268.0 0.1 reshape.102
  268.1 0.1 slice_reduce_fusion
  268.2 0.1 reshape_squeeze.3
  268.3 0.1 add.66
  268.4 0.9 convert_reduce_fusion
  269.3 0.1 select_reduce_fusion
  269.4 0.1 copy.20
  269.5 0.1 sub.7
  269.7 0.1 copy.21
  269.8 0.1 min.18
  269.9 8.6 %gather_fusion = bf16[128,2,128,128]{3,2,1,0:T(8,128)(2,1)} fusion(bf16[2,64,128,128]{3,2,1,0:T(8,128)(2,1)} %param.7, s32[1024]{0:T(1024)S(1)} %pad_clamp_fusion), kind=kCustom, calls=%fused_computation | custom fusion | bytes 16777728 | tf_op jit(solution)/shard_map/jit(_take)/gather | solution.py:48
  278.5 0.0 all-to-all-done
  278.5 14.6 %reshape.91 = bf16[128,2,128,128]{3,2,1,0:T(8,128)(2,1)} reshape(bf16[64,2,32768]{2,1,0:T(2,128)(2,1)} %all-to-all-done) | data formatting | bytes 16777216 | tf_op jit(solution)/shard_map/reshape | solution.py:47
  293.1 8.2 %fusion = f32[128,128,128,1]{2,1,3,0:T(8,128)S(1)} fusion(bf16[128,2,128,128]{3,2,1,0:T(8,128)(2,1)} %reshape.91, bf16[128,2,128,128]{3,2,1,0:T(8,128)(2,1)} %gather_fusion, pred[128]{0:T(512)(128)(4,1)S(1)} %compare_and_fusion), kind=kOutput, calls=%fused_computation.3 | convolution fusion | flops 1077936128 | bytes 25165952 | tf_op jit(solution)/shard_map/tnij,ntjk->nik/dot_general | solution.py:49
  301.3 9.7 %copy.41 = f32[16,8,128,128]{3,1,2,0:T(8,128)} copy(f32[16,8,128,128]{3,2,1,0:T(8,128)S(1)} %bitcast.38) | data formatting | bytes 16777216
  311.1 9.0 %copy.24 = f32[16384,128]{1,0:T(8,128)} copy(f32[16384,128]{0,1:T(8,128)} %bitcast.40) | data formatting | bytes 16777216 | tf_op jit(solution)/shard_map/dot_general | solution.py:53
  320.1 0.0 copy-start.1
  320.1 10.5 %fusion.15 = f32[64,128,128]{2,0,1:T(8,128)} fusion(f32[128,128,128]{2,1,0:T(8,128)} %bitcast.39, s32[128]{0:T(128)S(1)} %sub.7), kind=kOutput, calls=%fused_computation.25 | convolution fusion | flops 1610620928 | bytes 12583424 | tf_op jit(solution)/shard_map/dot_general | solution.py:53
  330.6 78.5 %all-reduce.1 = bf16[64,128,128]{2,0,1:T(8,128)(2,1)} all-reduce(f32[64,128,128]{2,0,1:T(8,128)} %fusion.15), channel_id=1, replica_groups=mesh['term'=4,'sector'=64] {'term'}, use_global_device_ids=true, to_apply=%region_3.4 | all-reduce | flops 1048576 | bytes 6291456 | tf_op jit(solution)/shard_map/psum | solution.py:59
  409.1 1.1 dynamic-slice_convert_fusion
  410.2 1.1 copy.25
  411.3 0.0 copy-done.1
  (8 shorter events, 0.1 us)
Async XLA Ops:
  0.0 1.6 copy-start
  36.3 13.5 %copy-start.2 = (s32[64,1]{0,1:T(1,128)S(1)}, s32[64,1]{0,1:T(1,128)}, u32[]{:S(2)}) copy-start(s32[64,1]{0,1:T(1,128)} %param.8) | copy-start | bytes 772
  36.3 13.5 %copy-start.3 = (s32[64,1]{0,1:T(1,128)S(1)}, s32[64,1]{0,1:T(1,128)}, u32[]{:S(2)}) copy-start(s32[64,1]{0,1:T(1,128)} %param.9) | copy-start | bytes 772
  36.3 242.3 %all-to-all-start = ((bf16[64,2,32768]{2,1,0:T(2,128)(2,1)}), bf16[64,2,32768]{2,1,0:T(2,128)(2,1)}, u32[]{:S(2)}, u32[]{:S(2)}) async-start(bf16[64,2,32768]{2,1,0:T(2,128)(2,1)} %reshape.90), calls=%async_computation | async-start | bytes 16777216 | tf_op jit(solution)/shard_map/all_to_all | solution.py:44
  320.1 91.3 %copy-start.1 = (bf16[64,128,128]{2,1,0:T(8,128)(2,1)S(1)}, bf16[64,128,128]{2,1,0:T(8,128)(2,1)}, u32[]{:S(2)}) copy-start(bf16[64,128,128]{2,1,0:T(8,128)(2,1)} %param.5) | copy-start | bytes 6291460
where the time goes:
time: 413 us; the launch traced here: 411 us
  blocking collectives  297 us (72%)
  local copies, waits for them, and re-layouts  65.4 us (16%)
  matrix products  32.8 us (8%)
  starting transfers between devices  13.5 us (3%)
    all_gather x1, blocking collectives, local(): lax.all_gather(jnp.concatenate([owner_map, left_local], axis=1), 'sector'...  218 us
    psum x1, blocking collectives, local(): total = lax.psum(partial_sum, 'term')  78.5 us
    reshape x1, local copies, waits for them, and re-layouts, local(): arrived = arrived.reshape(slots, terms_dev, width, width)  14.6 us
    reshape x1, local copies, waits for them, and re-layouts, local(): packed.reshape(n_sector, capacity, -1)  14.1 us
    all_to_all x1, starting transfers between devices, local(): lax.all_to_all(packed.reshape(n_sector, capacity, -1), 'sector', split_ax...  13.5 us
    dot_general x1, matrix products, local(): jnp.dot(collect, images.reshape(slots, -1), precision=lax.Precision.HIGHE...  10.5 us
    unnamed x10, local copies, waits for them, and re-layouts  9.9 us
    dot_general x1, local copies, waits for them, and re-layouts, local(): jnp.dot(collect, images.reshape(slots, -1), precision=lax.Precision.HIGHE...  8.99 us
  transfers between devices with their start and end apart: 1, of which 0 were waited for; matrix products, arithmetic and copies ran while one was open for 3% of the time, Pallas kernels for 0%

commit v1 on v0

v1 whole, which is shorter than its diff:
```python
import functools

import jax
import jax.numpy as jnp
from jax import lax
from jax.experimental import pallas as pl
from jax.experimental.pallas import tpu as pltpu
from jax.sharding import PartitionSpec as P

CAP = 2


def ranks_of(owners):
    count = owners.shape[-1]
    same = owners[..., :, None] == owners[..., None, :]
    earlier = lax.broadcasted_iota(jnp.int32, (count, count), 0) < lax.broadcasted_iota(
        jnp.int32, (count, count), 1
    )
    return jnp.sum((same & earlier).astype(jnp.int32), axis=-2)


def image_kernel(tags_ref, left_ref, arrived_ref, out_ref, acc):
    slots = arrived_ref.shape[0]
    acc[...] = jnp.zeros_like(acc)

    def step(i, carry):
        tag = tags_ref[i]

        @pl.when(tag >= 0)
        def _():
            lhs = jnp.concatenate([left_ref[0, tag], left_ref[1, tag]], axis=-1)
            acc[tag] += jnp.dot(lhs, arrived_ref[i], preferred_element_type=jnp.float32)

        return carry

    lax.fori_loop(0, slots, step, 0)
    out_ref[...] = acc[...].astype(out_ref.dtype)


def full_exchange(inter, slot_source, left_ops, tags):
    terms, sec_dev, width, _ = left_ops.shape
    packed = jnp.take(inter, slot_source, axis=0, mode="clip")
    arrived = lax.all_to_all(packed, "sector", split_axis=0, concat_axis=0, tiled=True)
    partial = pl.pallas_call(
        image_kernel,
        out_shape=jax.ShapeDtypeStruct((sec_dev, width, width), jnp.bfloat16),
        in_specs=[
            pl.BlockSpec(memory_space=pltpu.SMEM),
            pl.BlockSpec(memory_space=pltpu.VMEM),
            pl.BlockSpec(memory_space=pltpu.VMEM),
        ],
        out_specs=pl.BlockSpec(memory_space=pltpu.VMEM),
        scratch_shapes=[pltpu.VMEM((sec_dev, width, width), jnp.float32)],
        compiler_params=pltpu.CompilerParams(vmem_limit_bytes=48 << 20),
        name="images",
    )(tags, left_ops, arrived)
    total = lax.psum_scatter(
        partial.astype(jnp.float32), "term", scatter_dimension=1, tiled=True
    )
    return total.astype(jnp.bfloat16)


def local(psi_blocks, right_ops, left_ops, owner_map, left_local):
    sec_dev, width, _ = psi_blocks.shape
    terms = right_ops.shape[0]
    n_sector = lax.axis_size("sector")
    slots = n_sector * CAP
    owners = owner_map[:, 0]
    slot_id = owners * CAP + ranks_of(owners)
    hot = slot_id[None, :] == lax.broadcasted_iota(jnp.int32, (slots, sec_dev), 0)
    slot_source = jnp.sum(
        jnp.where(hot, lax.broadcasted_iota(jnp.int32, (slots, sec_dev), 1), 0), axis=1
    )
    routes = lax.all_gather(
        jnp.concatenate([owner_map, left_local], axis=1), "sector", axis=0, tiled=True
    )
    all_owners = routes[:, 0].reshape(n_sector, sec_dev)
    all_local = routes[:, 1].reshape(n_sector, sec_dev)
    mine = lax.axis_index("sector")
    all_ranks = ranks_of(all_owners)
    hits = (all_owners == mine)[:, :, None] & (
        all_ranks[:, :, None] == lax.broadcasted_iota(jnp.int32, (1, 1, CAP), 2)
    )
    tags = (jnp.sum(jnp.where(hits, all_local[:, :, None] + 1, 0), axis=1) - 1).reshape(slots)
    inter = (
        jnp.einsum("sij,tsjk->stik", psi_blocks, right_ops, preferred_element_type=jnp.float32)
        .astype(jnp.bfloat16)
        .reshape(sec_dev, terms * width, width)
    )
    return full_exchange(inter, slot_source, left_ops, tags)


def solution(mesh):
    placed = (
        P("sector", None, None),
        P("term", "sector", None, None),
        P("term", "sector", None, None),
        P("sector", None),
        P("sector", None),
    )
    return jax.shard_map(
        local, mesh=mesh, in_specs=placed, out_specs=P("sector", "term", None), check_vma=False
    )
```

time: 413 us -> 318 us (0.77)
  blocking collectives: 297 us -> 218 us
  local copies, waits for them, and re-layouts: 65.4 us -> 10.5 us
  waiting for transfers between devices: 0.01 us -> 40 us
  matrix products: 32.8 us -> 5.41 us
  Pallas kernels: 0 us -> 14.4 us
  between operations: 0.12 us -> 13.5 us
    psum x1 -> x0, blocking collectives: 78.5 us -> none  [local(): total = lax.psum(partial_sum, 'term')]
    reduce_scatter x0 -> x1, waiting for transfers between devices: none -> 40 us  [full_exchange(): lax.psum_scatter(partial.astype(jnp.float32), 'term', scatter_dimension=1...]
    reshape x2 -> x0, local copies, waits for them, and re-layouts: 28.7 us -> none  [the longest x1 14.6 us: local(): arrived = arrived.reshape(slots, terms_dev, width, width)]
    dot_general x3 -> x0, matrix products: 27.4 us -> none  [the longest x1 10.5 us: local(): jnp.dot(collect, images.reshape(slots, -1), precision=lax.Precision.HIGHE...]
    pallas_call x0 -> x1, Pallas kernels: none -> 14.4 us  [full_exchange(): pl.pallas_call(image_kernel, out_shape=jax.ShapeDtypeStruct((sec_dev, wid...]
    dot_general x1 -> x0, local copies, waits for them, and re-layouts: 8.99 us -> none  [local(): jnp.dot(collect, images.reshape(slots, -1), precision=lax.Precision.HIGHE...]
    convert_element_type x3 -> x0, local copies, waits for them, and re-layouts: 8.56 us -> none  [the longest x1 6.35 us: local(): inter = jnp.einsum('sij,tsjk->stik', psi_blocks, right_ops, preferred_ele...]
    unnamed x10 -> x9, local copies, waits for them, and re-layouts: 9.9 us -> 1.45 us
  transfers between devices with their start and end apart: 1 -> 2, of which waited for: 0 -> 1; matrix products, arithmetic and copies ran while one was open for 3% -> 0% of each run, Pallas kernels for 0% -> 0%
where the time goes in v1:
time: 318 us
  blocking collectives  218 us (69%)
  waiting for transfers between devices  40 us (13%)
  Pallas kernels  14.4 us (5%)
  starting transfers between devices  13.5 us (4%)
  between operations  13.5 us (4%)
  local copies, waits for them, and re-layouts  10.5 us (3%)
  matrix products  5.41 us (2%)
    all_gather x1, blocking collectives, local(): lax.all_gather(jnp.concatenate([owner_map, left_local], axis=1), 'sector'...  218 us
    reduce_scatter x1, waiting for transfers between devices, full_exchange(): lax.psum_scatter(partial.astype(jnp.float32), 'term', scatter_dimension=1...  40 us
    pallas_call x1, Pallas kernels, full_exchange(): pl.pallas_call(image_kernel, out_shape=jax.ShapeDtypeStruct((sec_dev, wid...  14.4 us
    all_to_all x1, starting transfers between devices, full_exchange(): lax.all_to_all(packed, 'sector', split_axis=0, concat_axis=0, tiled=True)  13.5 us
    gather x1, local copies, waits for them, and re-layouts, full_exchange(): packed = jnp.take(inter, slot_source, axis=0, mode='clip')  8.63 us
  transfers between devices with their start and end apart: 2, of which 1 were waited for; matrix products, arithmetic and copies ran while one was open for 0% of the time, Pallas kernels for 0%

profile of v1, /device:TPU:1, one launch (start us, length us, event | category | flops | bytes accessed | tf_op | source)
XLA Modules:
  0.0 318.1 jit_solution(5272297370440496585)
XLA Ops:
  6.5 0.0 copy-start
  6.5 0.9 convert_reduce_fusion.1
  7.5 0.7 multiply_add_fusion
  8.1 0.1 select_reduce_fusion.1
  8.2 0.0 copy-done
  8.2 5.4 %fusion.2 = bf16[64,2,128,128]{2,3,1,0:T(8,128)(2,1)} fusion(bf16[2,64,128,128]{3,2,1,0:T(8,128)(2,1)} %param.6, bf16[64,128,128]{2,1,0:T(8,128)(2,1)S(1)} %copy-done), kind=kOutput, calls=%fused_computation.3 | convolution fusion | flops 538968064 | bytes 10485760 | tf_op jit(solution)/shard_map/sij,tsjk->stik/dot_general | solution.py:86
  13.6 8.6 %gather_fusion = bf16[128,256,128]{2,1,0:T(8,128)(2,1)} fusion(bf16[64,256,128]{2,1,0:T(8,128)(2,1)} %bitcast.14, s32[1024]{0:T(1024)S(1)} %pad_clamp_fusion), kind=kCustom, calls=%fused_computation | custom fusion | bytes 16777728 | tf_op jit(solution)/shard_map/jit(_take)/gather | solution.py:42
  22.3 0.0 copy-start.2
  22.3 0.0 copy-start.3
  22.3 13.5 %all-to-all-start = ((bf16[128,256,128]{2,1,0:T(8,128)(2,1)}), bf16[128,256,128]{2,1,0:T(8,128)(2,1)}, u32[]{:S(2)}, u32[]{:S(2)}) async-start(bf16[128,256,128]{2,1,0:T(8,128)(2,1)} %gather_fusion), calls=%async_computation | async-start | bytes 16777216 | tf_op jit(solution)/shard_map/all_to_all | solution.py:43
  35.7 0.0 reduce-scatter.2.cloned.1.call-start
  35.8 0.0 copy-done.2
  35.8 0.0 copy-done.3
  35.8 218.2 %all-gather = s32[64,64,2]{1,2,0:T(2,128)S(1)} all-gather(s32[1,64,2]{1,2,0:T(2,128)S(1)} %add_bitcast_fusion), channel_id=1, replica_groups=mesh['term'=4,'sector'=64] {'sector'}, dimensions={0}, use_global_device_ids=true | all-gather | bytes 33280 | tf_op jit(solution)/shard_map/all_gather | solution.py:74
  254.0 0.1 reshape.51
  254.1 0.1 slice_reduce_fusion
  254.2 0.1 reshape_squeeze.3
  254.3 0.1 add.28
  254.4 0.7 convert_reduce_fusion
  255.1 0.1 select_reduce_fusion
  255.2 0.1 copy.12
  255.3 0.1 sub.7.tags_ref
  255.5 0.0 all-to-all-done.arrived_ref
  255.5 14.4 %images.1 = bf16[64,128,128]{2,1,0:T(8,128)(2,1)S(1)} custom-call(s32[128]{0:T(128)S(1)} %sub.7.tags_ref, bf16[2,64,128,128]{3,2,1,0:T(8,128)(2,1)} %left_ref.1, bf16[128,256,128]{2,1,0:T(8,128)(2,1)} %all-to-all-done.arrived_ref), custom_call_target="tpu_custom_call" | custom-call | tf_op jit(solution)/shard_map/images/pallas_call | solution.py:44
  269.9 0.0 copy-start.1
  269.9 1.3 copy-done.1
  271.3 0.0 reduce-scatter.2.cloned.1.call-update
  271.3 40.0 %reduce-scatter.2.cloned.1.call-done = bf16[64,32,128]{2,1,0:T(8,128)(2,1)} async-done(((bf16[64,128,128]{2,1,0:T(8,128)(2,1)}), bf16[64,32,128]{2,1,0:T(8,128)(2,1)}) %reduce-scatter.2.cloned.1.call-update) | async-done | bytes 524304 | tf_op jit(solution)/shard_map/reduce_scatter | solution.py:57
  (6 shorter events, 0.0 us)
Async XLA Ops:
  6.5 1.7 copy-start
  22.3 13.5 %copy-start.2 = (s32[64,1]{0,1:T(1,128)S(1)}, s32[64,1]{0,1:T(1,128)}, u32[]{:S(2)}) copy-start(s32[64,1]{0,1:T(1,128)} %param.9) | copy-start | bytes 772
  22.3 13.5 %copy-start.3 = (s32[64,1]{0,1:T(1,128)S(1)}, s32[64,1]{0,1:T(1,128)}, u32[]{:S(2)}) copy-start(s32[64,1]{0,1:T(1,128)} %param.8) | copy-start | bytes 772
  22.3 233.2 %all-to-all-start = ((bf16[128,256,128]{2,1,0:T(8,128)(2,1)}), bf16[128,256,128]{2,1,0:T(8,128)(2,1)}, u32[]{:S(2)}, u32[]{:S(2)}) async-start(bf16[128,256,128]{2,1,0:T(8,128)(2,1)} %gather_fusion), calls=%async_computation | async-start | bytes 16777216 | tf_op jit(solution)/shard_map/all_to_all | solution.py:43
  35.7 275.5 %reduce-scatter.2.cloned.1.call-start = ((), (), s32[]{:S(2)}) async-start(), calls=%async_computation.2 | async-start | bytes 2621440 | tf_op jit(solution)/shard_map/reduce_scatter | solution.py:57
  269.9 1.4 copy-start.1
Sparse Core Ops, SparseCore 0:
  271.4 39.7 reduce-scatter.1

commit v2 on v1

v2 whole, which is shorter than its diff:
```python
import functools

import jax
import jax.numpy as jnp
from jax import lax
from jax.experimental import pallas as pl
from jax.experimental.pallas import tpu as pltpu
from jax.sharding import PartitionSpec as P

MESH = pl.DeviceIdType.MESH
CAP = 2
NY, NZ, NC = 4, 8, 2
NX = 4
MEMBERS = NY * NC
REACH = (33, 24, 16, 7)
HOPS = len(REACH)


def chunk_bounds(hop):
    edges = [0, *reversed(REACH[hop - 1 :])]
    return list(zip(edges[:-1], edges[1:]))


def ranks_of(owners):
    count = owners.shape[-1]
    same = owners[..., :, None] == owners[..., None, :]
    earlier = lax.broadcasted_iota(jnp.int32, (count, count), 0) < lax.broadcasted_iota(
        jnp.int32, (count, count), 1
    )
    return jnp.sum((same & earlier).astype(jnp.int32), axis=-2)


def plan_of(owners, my_z):
    count = owners.shape[0]
    away = lax.rem(lax.rem(owners // NC, NZ) - my_z + NZ, NZ)
    counts = [jnp.sum((away == d).astype(jnp.int32)) for d in range(NZ)]
    up = [sum(counts[h:HOPS]) for h in range(1, HOPS)] + [0]
    down = [sum(counts[NZ - h] for h in range(k, HOPS)) for k in range(1, HOPS)] + [0]
    room_up = functools.reduce(jnp.minimum, [REACH[h] - up[h] for h in range(HOPS)])
    room_down = functools.reduce(jnp.minimum, [REACH[h] - down[h] for h in range(HOPS)])
    far_up = jnp.clip(room_up, 0, counts[HOPS])
    fits = (room_up >= 0) & (room_down >= counts[HOPS] - far_up)
    opposite = (away == HOPS).astype(jnp.int32)
    row = lax.broadcasted_iota(jnp.int32, (count, count), 0)
    col = lax.broadcasted_iota(jnp.int32, (count, count), 1)
    far_rank = jnp.sum(jnp.where(row < col, opposite[:, None], 0), axis=0)
    signed = jnp.where(
        away == HOPS,
        jnp.where(far_rank < far_up, -HOPS, HOPS),
        jnp.where(away < HOPS, -away, NZ - away),
    )
    key = signed * count + lax.iota(jnp.int32, count)
    position = jnp.sum((key[:, None] < key[None, :]).astype(jnp.int32), axis=0)
    order = jnp.sum(jnp.where(position[None, :] == row, col, 0), axis=1)
    return position, order, fits


def inter_kernel(order, route, psi, right, inter, routes, landing, send_sem, recv_sem):
    n = routes.shape[0]
    count = psi.shape[0]
    width = psi.shape[1]
    me = lax.axis_index("sector")
    barrier = pltpu.get_barrier_semaphore()

    def greet(o, carry):
        pl.semaphore_signal(
            barrier, inc=1, device_id={"sector": (me + o) % n}, device_id_type=MESH
        )
        return carry

    lax.fori_loop(1, n, greet, 0)

    def multiply(p, carry):
        s = order[p]
        both = jnp.concatenate([right[0, s], right[1, s]], axis=-1)
        made = jnp.dot(psi[s], both, preferred_element_type=jnp.float32).astype(inter.dtype)
        inter[p, :width] = made[:, :width]
        inter[p, width:] = made[:, width:]
        return carry

    lax.fori_loop(0, count // 2, multiply, 0, unroll=4)
    pl.semaphore_wait(barrier, n - 1)

    def copy_of(o):
        return pltpu.make_async_remote_copy(
            src_ref=route,
            dst_ref=landing.at[me],
            send_sem=send_sem.at[o],
            recv_sem=recv_sem.at[o],
            device_id={"sector": (me + o) % n},
            device_id_type=MESH,
        )

    def send(o, carry):
        copy_of(o).start()
        return carry

    lax.fori_loop(1, n, send, 0)
    lax.fori_loop(count // 2, count, multiply, 0, unroll=4)

    def finish(o, carry):
        copy_of(o).wait_send()
        copy_of(o).wait_recv()
        return carry

    lax.fori_loop(1, n, finish, 0)
    landing[me] = route[...]
    routes[...] = landing[...]


def ring_kernel(
    pick, tags, inter, left, out,
    up1, up2, up3, down1, down2, down3, far, outgoing, arrived, shares, taken,
    ring_send, ring_recv, row_send, row_recv, term_send, term_recv,
):
    count = inter.shape[0]
    width = inter.shape[2]
    tall = inter.shape[1]
    rows = out.shape[1]
    per_source = MEMBERS * CAP
    x = lax.axis_index("term")
    place = lax.axis_index("sector")
    c = place % NC
    z = (place // NC) % NZ
    y = place // (NC * NZ)
    my_member = y * NC + c

    def sector_id(yy, zz, cc):
        return {"sector": (yy * NZ + zz) * NC + cc}

    def member_of(j):
        return (y + j // NC) % NY, (c + j) % NC

    z_up, z_down = (z + 1) % NZ, (z + NZ - 1) % NZ
    barrier = pltpu.get_barrier_semaphore()
    pl.semaphore_signal(barrier, inc=1, device_id=sector_id(y, z_up, c), device_id_type=MESH)
    pl.semaphore_signal(barrier, inc=1, device_id=sector_id(y, z_down, c), device_id_type=MESH)
    for j in range(1, MEMBERS):
        yy, cc = member_of(j)
        pl.semaphore_signal(barrier, inc=1, device_id=sector_id(yy, z, cc), device_id_type=MESH)
    for d in range(1, NX):
        pl.semaphore_signal(barrier, inc=1, device_id={"term": (x + d) % NX}, device_id_type=MESH)
    pl.semaphore_wait(barrier, 2 + MEMBERS - 1 + NX - 1)

    reach_far = REACH[-1]
    up = (inter, up1, up2, up3, far)
    down = (inter, down1, down2, down3, far)
    number = {}
    for hop in range(1, HOPS + 1):
        for k in range(len(chunk_bounds(hop))):
            number[hop, k] = len(number)

    def ring_copy(way, hop, k):
        near, end = chunk_bounds(hop)[k]
        size = end - near
        if way == 0:
            source, target, neighbour = up[hop - 1], up[hop], z_up
            src_at, dst_at = near, near
        else:
            source, target, neighbour = down[hop - 1], down[hop], z_down
            held = count if hop == 1 else REACH[hop - 2]
            src_at = held - end
            dst_at = REACH[hop - 1] - end + (reach_far if hop == HOPS else 0)
        return pltpu.make_async_remote_copy(
            src_ref=source.at[pl.ds(src_at, size)],
            dst_ref=target.at[pl.ds(dst_at, size)],
            send_sem=ring_send.at[way, number[hop, k]],
            recv_sem=ring_recv.at[way, number[hop, k]],
            device_id=sector_id(y, neighbour, c),
            device_id_type=MESH,
        )

    def row_copy(d, j):
        yy, cc = member_of(j)
        return pltpu.make_async_remote_copy(
            src_ref=outgoing.at[d, j],
            dst_ref=arrived.at[(z + NZ - d) % NZ, my_member],
            send_sem=row_send.at[d, j],
            recv_sem=row_recv.at[d, j],
            device_id=sector_id(yy, z, cc),
            device_id_type=MESH,
        )

    def term_copy(d, dx):
        group = pl.ds(((z + NZ - d) % NZ) * per_source, per_source)
        return pltpu.make_async_remote_copy(
            src_ref=shares.at[dx - 1, group],
            dst_ref=taken.at[dx - 1, group],
            send_sem=term_send.at[d, dx],
            recv_sem=term_recv.at[d, dx],
            device_id={"term": (x + dx) % NX},
            device_id_type=MESH,
        )

    def hand_on(d, held):
        source = (z + NZ - d) % NZ

        def one(j, carry):
            yy, cc = member_of(j)
            entry = (source * MEMBERS + yy * NC + cc) * CAP
            outgoing[d, j, :tall] = held[pick[entry]]
            outgoing[d, j, tall:] = held[pick[entry + 1]]
            row_copy(d, j).start()
            return carry

        lax.fori_loop(1, MEMBERS, one, 0)
        entry = (source * MEMBERS + my_member) * CAP
        arrived[source, my_member, :tall] = held[pick[entry]]
        arrived[source, my_member, tall:] = held[pick[entry + 1]]

    def images(d):
        source = (z + NZ - d) % NZ

        def landed(j, carry):
            row_copy(d, j).wait_recv()
            return carry

        lax.fori_loop(1, MEMBERS, landed, 0)

        def one(m, carry):
            for r in range(CAP):
                slot = source * per_source + m * CAP + r
                tag = tags[slot]
                lhs = jnp.concatenate(
                    [
                        jnp.concatenate(
                            [left[t, tag, pl.ds(((x + dx) % NX) * rows, rows)] for dx in range(NX)],
                            axis=0,
                        )
                        for t in range(2)
                    ],
                    axis=1,
                )
                image = jnp.dot(
                    lhs,
                    arrived[source, m, r * tall : (r + 1) * tall],
                    preferred_element_type=jnp.float32,
                )
                out[slot] = image[:rows]
                for dx in range(1, NX):
                    shares[dx - 1, slot] = image[dx * rows : (dx + 1) * rows].astype(shares.dtype)
            return carry

        lax.fori_loop(0, MEMBERS, one, 0)
        for dx in range(1, NX):
            term_copy(d, dx).start()

    for k in range(len(chunk_bounds(1))):
        ring_copy(0, 1, k).start()
        ring_copy(1, 1, k).start()
    hand_on(0, inter)
    waiting = [0]
    for hop in range(1, HOPS + 1):
        pieces = len(chunk_bounds(hop))
        for k in range(pieces):
            for way in range(2):
                ring_copy(way, hop, k).wait_recv()
                if k < pieces - 1:
                    ring_copy(way, hop + 1, k).start()
        if hop < HOPS:
            hand_on(hop, up[hop])
            hand_on(NZ - hop, down[hop])
            arriving = [hop, NZ - hop]
        else:
            hand_on(hop, far)
            arriving = [hop]
        for d in waiting:
            images(d)
        waiting = arriving
    for d in waiting:
        images(d)

    def settle(d, carry):
        for dx in range(1, NX):
            term_copy(d, dx).wait_recv()
        return carry

    lax.fori_loop(0, NZ, settle, 0)

    def total(slot, carry):
        out[slot] = out[slot] + (
            taken[0, slot].astype(jnp.float32)
            + taken[1, slot].astype(jnp.float32)
            + taken[2, slot].astype(jnp.float32)
        )
        return carry

    lax.fori_loop(0, out.shape[0], total, 0, unroll=4)

    for way in range(2):
        for hop, k in number:
            ring_copy(way, hop, k).wait_send()

    def sent(d, carry):
        for j in range(1, MEMBERS):
            row_copy(d, j).wait_send()
        for dx in range(1, NX):
            term_copy(d, dx).wait_send()
        return carry

    lax.fori_loop(0, NZ, sent, 0)


def gather_kernel(tags, found, out, acc):
    acc[...] = jnp.zeros_like(acc)

    def step(i, carry):
        tag = tags[i]

        @pl.when(tag >= 0)
        def _():
            acc[tag] += found[i]

        return carry

    lax.fori_loop(0, found.shape[0], step, 0)
    out[...] = acc[...].astype(out.dtype)


def image_kernel(tags_ref, left_ref, arrived_ref, out_ref, acc):
    slots = arrived_ref.shape[0]
    acc[...] = jnp.zeros_like(acc)

    def step(i, carry):
        tag = tags_ref[i]

        @pl.when(tag >= 0)
        def _():
            lhs = jnp.concatenate([left_ref[0, tag], left_ref[1, tag]], axis=-1)
            acc[tag] += jnp.dot(lhs, arrived_ref[i], preferred_element_type=jnp.float32)

        return carry

    lax.fori_loop(0, slots, step, 0)
    out_ref[...] = acc[...].astype(out_ref.dtype)


def full_exchange(inter, slot_source, left_ops, tags):
    terms, sec_dev, width, _ = left_ops.shape
    packed = jnp.take(inter, slot_source, axis=0, mode="clip")
    arrived = lax.all_to_all(packed, "sector", split_axis=0, concat_axis=0, tiled=True)
    partial = pl.pallas_call(
        image_kernel,
        out_shape=jax.ShapeDtypeStruct((sec_dev, width, width), jnp.float32),
        in_specs=[
            pl.BlockSpec(memory_space=pltpu.SMEM),
            pl.BlockSpec(memory_space=pltpu.VMEM),
            pl.BlockSpec(memory_space=pltpu.VMEM),
        ],
        out_specs=pl.BlockSpec(memory_space=pltpu.VMEM),
        scratch_shapes=[pltpu.VMEM((sec_dev, width, width), jnp.float32)],
        compiler_params=pltpu.CompilerParams(vmem_limit_bytes=48 << 20),
        name="images",
    )(tags, left_ops, arrived)
    total = lax.psum_scatter(partial, "term", scatter_dimension=1, tiled=True)
    return total.astype(jnp.bfloat16)


def ring_exchange(inter, pick, tags, left_ops):
    terms, sec_dev, width, _ = left_ops.shape
    tall = inter.shape[1]
    slots = tags.shape[0]
    rows = width // NX
    smem = pl.BlockSpec(memory_space=pltpu.SMEM)
    vmem = pl.BlockSpec(memory_space=pltpu.VMEM)
    dma = pltpu.SemaphoreType.DMA
    pieces = sum(range(1, HOPS + 1))
    found = pl.pallas_call(
        ring_kernel,
        out_shape=jax.ShapeDtypeStruct((slots, rows, width), jnp.float32),
        in_specs=[smem, smem, vmem, vmem],
        out_specs=vmem,
        scratch_shapes=[
            pltpu.VMEM((REACH[0], tall, width), jnp.bfloat16),
            pltpu.VMEM((REACH[1], tall, width), jnp.bfloat16),
            pltpu.VMEM((REACH[2], tall, width), jnp.bfloat16),
            pltpu.VMEM((REACH[0], tall, width), jnp.bfloat16),
            pltpu.VMEM((REACH[1], tall, width), jnp.bfloat16),
            pltpu.VMEM((REACH[2], tall, width), jnp.bfloat16),
            pltpu.VMEM((2 * REACH[3], tall, width), jnp.bfloat16),
            pltpu.VMEM((NZ, MEMBERS, CAP * tall, width), jnp.bfloat16),
            pltpu.VMEM((NZ, MEMBERS, CAP * tall, width), jnp.bfloat16),
            pltpu.VMEM((NX - 1, slots, rows, width), jnp.bfloat16),
            pltpu.VMEM((NX - 1, slots, rows, width), jnp.bfloat16),
            dma((2, pieces)),
            dma((2, pieces)),
            dma((NZ, MEMBERS)),
            dma((NZ, MEMBERS)),
            dma((NZ, NX)),
            dma((NZ, NX)),
        ],
        compiler_params=pltpu.CompilerParams(
            collective_id=1, has_side_effects=True, vmem_limit_bytes=62 << 20
        ),
        name="ring",
    )(pick, jnp.maximum(tags, 0), inter, left_ops)
    return pl.pallas_call(
        gather_kernel,
        out_shape=jax.ShapeDtypeStruct((sec_dev, rows, width), jnp.bfloat16),
        in_specs=[smem, vmem],
        out_specs=vmem,
        scratch_shapes=[pltpu.VMEM((sec_dev, rows, width), jnp.float32)],
        name="gather",
    )(tags, found)


def local(psi_blocks, right_ops, left_ops, owner_map, left_local):
    sec_dev, width, _ = psi_blocks.shape
    terms = right_ops.shape[0]
    n_sector = lax.axis_size("sector")
    slots = n_sector * CAP
    mine = lax.axis_index("sector")
    my_c, my_z, my_y = mine % NC, (mine // NC) % NZ, mine // (NC * NZ)
    owners = owner_map[:, 0]
    ranks = ranks_of(owners)
    position, order, fits = plan_of(owners, my_z)
    route = jnp.concatenate(
        [owners, left_local[:, 0], jnp.where(fits, position, -1), ranks]
    ).reshape(2, 2 * sec_dev)

    smem = pl.BlockSpec(memory_space=pltpu.SMEM)
    vmem = pl.BlockSpec(memory_space=pltpu.VMEM)
    inter, routes = pl.pallas_call(
        inter_kernel,
        out_shape=(
            jax.ShapeDtypeStruct((sec_dev, terms * width, width), jnp.bfloat16),
            jax.ShapeDtypeStruct((n_sector, 2, 2 * sec_dev), jnp.int32),
        ),
        in_specs=[smem, vmem, vmem, vmem],
        out_specs=(vmem, vmem),
        scratch_shapes=[
            pltpu.VMEM((n_sector, 2, 2 * sec_dev), jnp.int32),
            pltpu.SemaphoreType.DMA((n_sector,)),
            pltpu.SemaphoreType.DMA((n_sector,)),
        ],
        compiler_params=pltpu.CompilerParams(
            collective_id=0, has_side_effects=True, vmem_limit_bytes=48 << 20
        ),
        name="inter",
    )(order, route, psi_blocks, right_ops)

    routes = routes.reshape(n_sector, 4, sec_dev)
    all_owners, all_local, all_positions, all_ranks = (routes[:, k] for k in range(4))
    all_fit = jnp.min(all_positions) >= 0

    hits = (all_owners == mine)[:, None, :] & (
        all_ranks[:, None, :] == lax.broadcasted_iota(jnp.int32, (1, CAP, 1), 1)
    )
    tags = jnp.sum(jnp.where(hits, all_local[:, None, :] + 1, 0), axis=2) - 1

    ring = lax.dynamic_index_in_dim(
        lax.dynamic_index_in_dim(
            routes.reshape(NY, NZ, NC, 4, sec_dev), my_y, axis=0, keepdims=False
        ),
        my_c,
        axis=1,
        keepdims=False,
    )
    member = lax.broadcasted_iota(jnp.int32, (1, MEMBERS, 1, 1), 1)
    goal = ((member // NC) * NZ + my_z) * NC + member % NC
    for_member = (ring[:, None, None, 0] == goal) & (
        ring[:, None, None, 3] == lax.broadcasted_iota(jnp.int32, (1, 1, CAP, 1), 2)
    )
    back = lax.rem(my_z - lax.iota(jnp.int32, NZ) + NZ, NZ)
    start = jnp.zeros_like(back)
    for h in range(1, HOPS):
        start = jnp.where(back == NZ - h, sec_dev - REACH[h - 1], start)
    place = ring[:, 2] - start[:, None]
    place = jnp.where(
        (back[:, None] == HOPS) & (place >= REACH[-1]), place - (sec_dev - 2 * REACH[-1]), place
    )
    pick = jnp.sum(jnp.where(for_member, place[:, None, None, :], 0), axis=3).reshape(slots)

    def by_ring(inter, left_ops):
        spread = tags.reshape(NY, NZ, NC, CAP).transpose(1, 0, 2, 3).reshape(slots)
        return ring_exchange(inter, pick, spread, left_ops)

    def by_all(inter, left_ops):
        slot_id = owners * CAP + ranks
        hot = slot_id[None, :] == lax.broadcasted_iota(jnp.int32, (slots, sec_dev), 0)
        slot_source = jnp.sum(jnp.where(hot, position[None, :], 0), axis=1)
        return full_exchange(inter, slot_source, left_ops, tags.reshape(slots))

    return lax.cond(all_fit, by_ring, by_all, inter, left_ops)


def solution(mesh):
    placed = (
        P("sector", None, None),
        P("term", "sector", None, None),
        P("term", "sector", None, None),
        P("sector", None),
        P("sector", None),
    )
    return jax.shard_map(
        local, mesh=mesh, in_specs=placed, out_specs=P("sector", "term", None), check_vma=False
    )
```

time: 318 us -> 220 us (0.69)
  blocking collectives: 218 us -> 0 us
  Pallas kernels: 14.4 us -> 187 us
  waiting for transfers between devices: 40 us -> 0 us
  starting transfers between devices: 13.5 us -> 0 us
  between operations: 13.5 us -> 22.9 us
  local copies, waits for them, and re-layouts: 10.5 us -> 4.07 us
  matrix products: 5.41 us -> 0 us
  other arithmetic: 2.62 us -> 6.02 us
    all_gather x1 -> x0, blocking collectives: 218 us -> none  [local(): lax.all_gather(jnp.concatenate([owner_map, left_local], axis=1), 'sector'...]
    pallas_call x1 -> x3, Pallas kernels: 14.4 us -> 187 us  [the longest x1 162 us: ring_exchange(): pl.pallas_call(ring_kernel, out_shape=jax.ShapeDtypeStruct((slots, rows,...]
    reduce_scatter x1 -> x0, waiting for transfers between devices: 40 us -> none  [full_exchange(): lax.psum_scatter(partial.astype(jnp.float32), 'term', scatter_dimension=1...]
    all_to_all x1 -> x0, starting transfers between devices: 13.5 us -> none  [full_exchange(): lax.all_to_all(packed, 'sector', split_axis=0, concat_axis=0, tiled=True)]
    gather x1 -> x0, local copies, waits for them, and re-layouts: 8.63 us -> none  [full_exchange(): packed = jnp.take(inter, slot_source, axis=0, mode='clip')]
    dot_general x1 -> x0, matrix products: 5.41 us -> none  [local(): jnp.einsum('sij,tsjk->stik', psi_blocks, right_ops, preferred_element_typ...]
  transfers between devices with their start and end apart: 2 -> 0, of which waited for: 1 -> 0; matrix products, arithmetic and copies ran while one was open for 0% -> 0% of each run, Pallas kernels for 0% -> 0%
where the time goes in v2:
time: 220 us
  Pallas kernels  187 us (85%)
  between operations  22.9 us (10%)
  other arithmetic  6.02 us (3%)
  local copies, waits for them, and re-layouts  4.07 us (2%)
    pallas_call x1, Pallas kernels, ring_exchange(): pl.pallas_call(ring_kernel, out_shape=jax.ShapeDtypeStruct((slots, rows,...  162 us
    pallas_call x1, Pallas kernels, local(): pl.pallas_call(inter_kernel, out_shape=(jax.ShapeDtypeStruct((sec_dev, te...  21.8 us

profile of v2, /device:TPU:1, one launch (start us, length us, event | category | flops | bytes accessed | tf_op | source)
XLA Modules:
  0.0 220.1 jit_solution(12337895213453625143)
XLA Ops:
  6.5 0.0 copy-start.3
  6.5 1.5 fusion.18
  16.8 0.7 fusion.7
  17.5 0.1 select_reduce_fusion.4
  17.6 0.8 convert_reduce_fusion
  18.4 0.8 add_bitcast_fusion.route
  19.2 0.1 select_reduce_fusion.3.order
  19.3 0.0 copy-start.1
  19.3 1.6 copy-done.1
  20.9 21.8 %inter.1 = (bf16[64,256,128]{2,1,0:T(8,128)(2,1)}, s32[64,2,128]{2,1,0:T(2,128)S(1)}) custom-call(s32[64]{0:T(128)S(1)} %select_reduce_fusion.3.order, s32[2,128]{1,0:T(2,128)S(1)} %add_bitcast_fusion.route, bf16[64,128,128]{2,1,0:T(8,128)(2,1)S(1)} %copy-done.1, bf16[2,64,128,128]{3,2,1,0:T(8,128)(2,1)} %right.1), custom_call_target="tpu_custom_call" | custom-call | tf_op jit(solution)/shard_map/inter/pallas_call | solution.py:423
  42.7 0.1 reshape.232
  42.9 0.8 fusion.28
  43.7 0.1 select_reduce_fusion.2
  44.5 0.0 copy-done.3
  44.6 167.9 %conditional.1 = (bf16[64,32,128]{2,1,0:T(8,128)(2,1)S(1)}) conditional(s32[]{:T(128)} %convert_element_type.44, (s32[64,2]{0,1:T(2,128)S(1)}, s32[64]{0:T(128)S(1)}, s32[64]{0:T(128)S(1)}, s32[64]{0:T(128)S(1)}, bf16[64,256,128]{2,1,0:T(8,128)(2,1)}, /*index=5*/bf16[2,64,128,128]{3,2,1,0:T(8,128)(2,1)}) %tuple.91, (s32[64,2]{0,1:T(2,128)S(1)}, ...), branch_computations={%region_13.16_spmd, %region_16.18_spmd} | conditional | flops 287744 | bytes 76030824 | solution.py:484
  44.6 0.1 reshape_reshape.3
  44.8 0.1 broadcast_compare_fusion
  44.9 0.1 add_select_fusion
  45.0 0.4 select_reduce_fusion
  45.4 0.1 copy.17
  45.5 0.7 reshape.228.pick
  46.2 0.1 reshape.226
  46.3 0.3 copy.15
  46.6 0.1 reshape.227.tags
  46.8 0.0 copy-start.4
  46.8 0.5 broadcast_maximum_fusion.tags
  47.3 161.6 %ring.1.found = f32[128,32,128]{2,1,0:T(8,128)} custom-call(s32[128]{0:T(128)} %reshape.228.pick, s32[128]{0:T(128)} %broadcast_maximum_fusion.tags, bf16[64,256,128]{2,1,0:T(8,128)(2,1)} %get-tuple-element.249.inter, bf16[2,64,128,128]{3,2,1,0:T(8,128)(2,1)} %get-tuple-element.250.left), custom_call_target="tpu_custom_call" | custom-call | tf_op jit(solution)/shard_map/cond/branch_1_fun/ring/pallas_call | solution.py:368
  208.9 0.0 copy-done.4
  209.0 3.5 %gather.7 = bf16[64,32,128]{2,1,0:T(8,128)(2,1)S(1)} custom-call(s32[128]{0:T(128)} %copy-done.4, f32[128,32,128]{2,1,0:T(8,128)} %ring.1.found), custom_call_target="tpu_custom_call" | custom-call | tf_op jit(solution)/shard_map/cond/branch_1_fun/gather/pallas_call | solution.py:397
  212.5 0.0 copy-start.2
  212.5 0.8 copy-done.2
  (16 shorter events, 0.1 us)
Async XLA Ops:
  6.5 38.0 %copy-start.3 = (s32[64,1]{0,1:T(1,128)S(1)}, s32[64,1]{0,1:T(1,128)}, u32[]{:S(2)}) copy-start(s32[64,1]{0,1:T(1,128)} %param.10) | copy-start | bytes 772
  19.3 1.6 copy-start.1
  46.8 162.2 %copy-start.4 = (s32[128]{0:T(128)}, s32[128]{0:T(128)S(1)}, u32[]{:S(2)}) copy-start(s32[128]{0:T(128)S(1)} %reshape.227.tags) | copy-start | bytes 1540 | tf_op jit(solution)/shard_map/cond
  212.5 0.8 copy-start.2

commit v3 on v2

v3 whole, which is shorter than its diff:
```python
import functools

import jax
import jax.numpy as jnp
from jax import lax
from jax.experimental import pallas as pl
from jax.experimental.pallas import tpu as pltpu
from jax.sharding import PartitionSpec as P

MESH = pl.DeviceIdType.MESH
CAP = 2
NY, NZ, NC = 4, 8, 2
NX = 4
MEMBERS = NY * NC
REACH = (33, 24, 16, 7)
HOPS = len(REACH)


def chunk_bounds(hop):
    edges = [0, *reversed(REACH[hop - 1 :])]
    return list(zip(edges[:-1], edges[1:]))


def ranks_of(owners):
    count = owners.shape[-1]
    same = owners[..., :, None] == owners[..., None, :]
    earlier = lax.broadcasted_iota(jnp.int32, (count, count), 0) < lax.broadcasted_iota(
        jnp.int32, (count, count), 1
    )
    return jnp.sum((same & earlier).astype(jnp.int32), axis=-2)


def plan_of(owners, my_z):
    count = owners.shape[0]
    away = lax.rem(lax.rem(owners // NC, NZ) - my_z + NZ, NZ)
    counts = [jnp.sum((away == d).astype(jnp.int32)) for d in range(NZ)]
    up = [sum(counts[h:HOPS]) for h in range(1, HOPS)] + [0]
    down = [sum(counts[NZ - h] for h in range(k, HOPS)) for k in range(1, HOPS)] + [0]
    room_up = functools.reduce(jnp.minimum, [REACH[h] - up[h] for h in range(HOPS)])
    room_down = functools.reduce(jnp.minimum, [REACH[h] - down[h] for h in range(HOPS)])
    far_up = jnp.clip(room_up, 0, counts[HOPS])
    fits = (room_up >= 0) & (room_down >= counts[HOPS] - far_up)
    opposite = (away == HOPS).astype(jnp.int32)
    row = lax.broadcasted_iota(jnp.int32, (count, count), 0)
    col = lax.broadcasted_iota(jnp.int32, (count, count), 1)
    far_rank = jnp.sum(jnp.where(row < col, opposite[:, None], 0), axis=0)
    signed = jnp.where(
        away == HOPS,
        jnp.where(far_rank < far_up, -HOPS, HOPS),
        jnp.where(away < HOPS, -away, NZ - away),
    )
    key = signed * count + lax.iota(jnp.int32, count)
    position = jnp.sum((key[:, None] < key[None, :]).astype(jnp.int32), axis=0)
    order = jnp.sum(jnp.where(position[None, :] == row, col, 0), axis=1)
    return position, order, fits


def tables_of(owners, ranks, left_local, position, fits, my_z):
    count = owners.shape[0]
    shape = (NZ, MEMBERS * CAP, count)
    mate = lax.broadcasted_iota(jnp.int32, shape, 0)
    member = lax.broadcasted_iota(jnp.int32, shape, 1) // CAP
    rank = lax.broadcasted_iota(jnp.int32, shape, 1) % CAP
    goal = ((member // NC) * NZ + mate) * NC + member % NC
    hits = (owners == goal) & (ranks == rank)
    ahead = lax.rem(lax.iota(jnp.int32, NZ) - my_z + NZ, NZ)[:, None]
    start, size = jnp.zeros_like(ahead), jnp.full_like(ahead, count)
    for h in range(1, HOPS):
        start = jnp.where(ahead == NZ - h, count - REACH[h - 1], start)
        size = jnp.where((ahead == h) | (ahead == NZ - h), REACH[h - 1], size)
    size = jnp.where(ahead == HOPS, 2 * REACH[-1], size)
    where = jnp.sum(jnp.where(hits, position, 0), axis=2) - start
    where = jnp.where(
        (ahead == HOPS) & (where >= REACH[-1]), where - (count - 2 * REACH[-1]), where
    )
    where = jnp.clip(where, 0, size - 1)
    tags = jnp.sum(jnp.where(hits, left_local + 1, 0), axis=2) - 1
    flag = jnp.broadcast_to(fits.astype(jnp.int32), (NZ, 128 - 2 * MEMBERS * CAP))
    return jnp.concatenate([where, tags, flag], axis=1).reshape(NZ, 1, 128)


def ring_kernel(
    order, table, psi_far, right_far, left_far, out, all_tables,
    psi, right, left, inter0, inter1,
    up10, up20, up30, down10, down20, down30, far0,
    up11, up21, up31, down11, down21, down31, far1,
    outgoing, arrived, shares, taken, mates, picks, rowmates, tags,
    load, local_sem, ring_send, ring_recv, row_send, row_recv, term_send, term_recv,
    mate_send, mate_recv, table_send, table_recv,
):
    count, width = psi.shape[0], psi.shape[1]
    rows = out.shape[1]
    per_source = MEMBERS * CAP
    x = lax.axis_index("term")
    place = lax.axis_index("sector")
    c = place % NC
    z = (place // NC) % NZ
    y = place // (NC * NZ)
    my_member = y * NC + c

    def sector_id(yy, zz, cc):
        return {"sector": (yy * NZ + zz) * NC + cc}

    def member_of(j):
        return (y + j // NC) % NY, (c + j) % NC

    z_up, z_down = (z + 1) % NZ, (z + NZ - 1) % NZ
    loads = [
        pltpu.make_async_copy(psi_far, psi, load.at[0]),
        pltpu.make_async_copy(right_far, right, load.at[1]),
        pltpu.make_async_copy(left_far, left, load.at[2]),
    ]
    for copy in loads:
        copy.start()
    own_row = pltpu.make_async_copy(table.at[z], mates.at[z], local_sem.at[0])
    own_row.start()
    barrier = pltpu.get_barrier_semaphore()
    for d in range(1, NZ):
        pl.semaphore_signal(
            barrier, inc=1, device_id=sector_id(y, (z + d) % NZ, c), device_id_type=MESH
        )
    for j in range(1, MEMBERS):
        yy, cc = member_of(j)
        pl.semaphore_signal(barrier, inc=1, device_id=sector_id(yy, z, cc), device_id_type=MESH)
    for d in range(1, NX):
        pl.semaphore_signal(barrier, inc=1, device_id={"term": (x + d) % NX}, device_id_type=MESH)

    inter = (inter0, inter1)
    up = ((inter0, up10, up20, up30, far0), (inter1, up11, up21, up31, far1))
    down = ((inter0, down10, down20, down30, far0), (inter1, down11, down21, down31, far1))
    reach_far = REACH[-1]
    number = {}
    for hop in range(1, HOPS + 1):
        for k in range(len(chunk_bounds(hop))):
            number[hop, k] = len(number)

    def ring_copy(w, way, hop, k):
        near, end = chunk_bounds(hop)[k]
        size = end - near
        if way == 0:
            source, target, neighbour = up[w][hop - 1], up[w][hop], z_up
            src_at, dst_at = near, near
        else:
            source, target, neighbour = down[w][hop - 1], down[w][hop], z_down
            held = count if hop == 1 else REACH[hop - 2]
            src_at = held - end
            dst_at = REACH[hop - 1] - end + (reach_far if hop == HOPS else 0)
        return pltpu.make_async_remote_copy(
            src_ref=source.at[pl.ds(src_at, size)],
            dst_ref=target.at[pl.ds(dst_at, size)],
            send_sem=ring_send.at[w, way, number[hop, k]],
            recv_sem=ring_recv.at[w, way, number[hop, k]],
            device_id=sector_id(y, neighbour, c),
            device_id_type=MESH,
        )

    def row_copy(w, d, j):
        yy, cc = member_of(j)
        return pltpu.make_async_remote_copy(
            src_ref=outgoing.at[w, d, j],
            dst_ref=arrived.at[w, (z + NZ - d) % NZ, my_member],
            send_sem=row_send.at[w, d, j],
            recv_sem=row_recv.at[w, d, j],
            device_id=sector_id(yy, z, cc),
            device_id_type=MESH,
        )

    def term_copy(d, dx):
        group = pl.ds(((z + NZ - d) % NZ) * per_source, per_source)
        return pltpu.make_async_remote_copy(
            src_ref=shares.at[dx - 1, group],
            dst_ref=taken.at[dx - 1, group],
            send_sem=term_send.at[d, dx],
            recv_sem=term_recv.at[d, dx],
            device_id={"term": (x + dx) % NX},
            device_id_type=MESH,
        )

    def mate_copy(d):
        mate = (z + d) % NZ
        return pltpu.make_async_remote_copy(
            src_ref=table.at[mate],
            dst_ref=mates.at[z],
            send_sem=mate_send.at[d],
            recv_sem=mate_recv.at[d],
            device_id=sector_id(y, mate, c),
            device_id_type=MESH,
        )

    def table_copy(j):
        yy, cc = member_of(j)
        return pltpu.make_async_remote_copy(
            src_ref=mates,
            dst_ref=rowmates.at[my_member],
            send_sem=table_send.at[j],
            recv_sem=table_recv.at[j],
            device_id=sector_id(yy, z, cc),
            device_id_type=MESH,
        )

    def multiply(p, carry):
        s = order[p]
        both = jnp.concatenate([right[0, s], right[1, s]], axis=-1)
        made = jnp.dot(psi[s], both, preferred_element_type=jnp.float32).astype(inter0.dtype)
        inter0[p] = made[:, :width]
        inter1[p] = made[:, width:]
        return carry

    def hand_on(w, d, held):
        source = (z + NZ - d) % NZ

        def one(j, carry):
            yy, cc = member_of(j)
            entry = (yy * NC + cc) * CAP
            outgoing[w, d, j, :width] = held[picks[source, 0, entry]]
            outgoing[w, d, j, width:] = held[picks[source, 0, entry + 1]]
            row_copy(w, d, j).start()
            return carry

        lax.fori_loop(1, MEMBERS, one, 0)
        entry = my_member * CAP
        arrived[w, source, my_member, :width] = held[picks[source, 0, entry]]
        arrived[w, source, my_member, width:] = held[picks[source, 0, entry + 1]]

    def images(d):
        source = (z + NZ - d) % NZ

        def landed(j, carry):
            row_copy(0, d, j).wait_recv()
            row_copy(1, d, j).wait_recv()
            return carry

        lax.fori_loop(1, MEMBERS, landed, 0)

        def one(m, carry):
            for r in range(CAP):
                slot = source * per_source + m * CAP + r
                tag = jnp.maximum(tags[m, source, 0, per_source + my_member * CAP + r], 0)
                lhs = jnp.concatenate(
                    [
                        jnp.concatenate(
                            [left[t, tag, pl.ds(((x + dx) % NX) * rows, rows)] for dx in range(NX)],
                            axis=0,
                        )
                        for t in range(2)
                    ],
                    axis=1,
                )
                rhs = jnp.concatenate(
                    [arrived[t, source, m, r * width : (r + 1) * width] for t in range(2)], axis=0
                )
                image = jnp.dot(lhs, rhs, preferred_element_type=jnp.float32)
                out[slot] = image[:rows]
                for dx in range(1, NX):
                    shares[dx - 1, slot] = image[dx * rows : (dx + 1) * rows].astype(shares.dtype)
            return carry

        lax.fori_loop(0, MEMBERS, one, 0)
        for dx in range(1, NX):
            term_copy(d, dx).start()

    loads[0].wait()
    loads[1].wait()
    edges = [0, *reversed(REACH)]
    spans = [
        [(edges[k], edges[k + 1]), (count - edges[k + 1], count - edges[k])] for k in range(HOPS)
    ]
    spans[-1] = [(edges[HOPS - 1], count - edges[HOPS - 1])]
    for k in range(HOPS):
        for low, high in spans[k]:
            lax.fori_loop(low, high, multiply, 0, unroll=True)
        if k == 0:
            pl.semaphore_wait(barrier, NZ - 1 + MEMBERS - 1 + NX - 1)
            for d in range(1, NZ):
                mate_copy(d).start()
        ring_copy(0, 0, 1, k).start()
        ring_copy(0, 1, 1, k).start()

    own_row.wait()
    for d in range(1, NZ):
        mate_copy(d).wait_recv()
    for j in range(1, MEMBERS):
        table_copy(j).start()
    to_picks = pltpu.make_async_copy(mates, picks, local_sem.at[1])
    to_picks.start()
    own_rows = pltpu.make_async_copy(mates, rowmates.at[my_member], local_sem.at[2])
    own_rows.start()
    to_picks.wait()
    for w in range(2):
        hand_on(w, 0, inter[w])
    own_rows.wait()
    for j in range(1, MEMBERS):
        table_copy(j).wait_recv()
    to_tags = pltpu.make_async_copy(rowmates, tags, local_sem.at[3])
    to_tags.start()
    to_tags.wait()
    for m in range(MEMBERS):
        all_tables[m] = rowmates[m]
    loads[2].wait()

    waiting = [0]
    for w in range(2):
        for hop in range(1, HOPS + 1):
            pieces = len(chunk_bounds(hop))
            for k in range(pieces):
                for way in range(2):
                    ring_copy(w, way, hop, k).wait_recv()
                if k < pieces - 1:
                    between = w == 0 and hop == HOPS - 1
                    if between:
                        for late in range(HOPS - 1):
                            ring_copy(1, 0, 1, late).start()
                            ring_copy(1, 1, 1, late).start()
                    ring_copy(w, 0, hop + 1, k).start()
                    ring_copy(w, 1, hop + 1, k).start()
                    if between:
                        ring_copy(1, 0, 1, HOPS - 1).start()
                        ring_copy(1, 1, 1, HOPS - 1).start()
            if hop < HOPS:
                hand_on(w, hop, up[w][hop])
                hand_on(w, NZ - hop, down[w][hop])
                arriving = [hop, NZ - hop]
            else:
                hand_on(w, hop, up[w][hop])
                arriving = [hop]
            for d in waiting:
                images(d)
            waiting = arriving if w == 1 else []
    for d in waiting:
        images(d)

    def settle(d, carry):
        for dx in range(1, NX):
            term_copy(d, dx).wait_recv()
        return carry

    lax.fori_loop(0, NZ, settle, 0)

    def total(slot, carry):
        out[slot] = out[slot] + (
            taken[0, slot].astype(jnp.float32)
            + taken[1, slot].astype(jnp.float32)
            + taken[2, slot].astype(jnp.float32)
        )
        return carry

    lax.fori_loop(0, out.shape[0], total, 0, unroll=4)

    for w in range(2):
        for way in range(2):
            for hop, k in number:
                ring_copy(w, way, hop, k).wait_send()
    for d in range(1, NZ):
        mate_copy(d).wait_send()
    for j in range(1, MEMBERS):
        table_copy(j).wait_send()

    def sent(d, carry):
        for j in range(1, MEMBERS):
            row_copy(0, d, j).wait_send()
            row_copy(1, d, j).wait_send()
        for dx in range(1, NX):
            term_copy(d, dx).wait_send()
        return carry

    lax.fori_loop(0, NZ, sent, 0)


def gather_kernel(me, tables, found, out, acc):
    acc[...] = jnp.zeros_like(acc)
    column = (MEMBERS + me[0]) * CAP

    def step(i, carry):
        tag = tables[((i // CAP) % MEMBERS) * NZ + i // (MEMBERS * CAP), 0, column + i % CAP]

        @pl.when(tag >= 0)
        def _():
            acc[tag] += found[i]

        return carry

    lax.fori_loop(0, found.shape[0], step, 0)
    out[...] = acc[...].astype(out.dtype)


def image_kernel(tags_ref, left_ref, arrived_ref, out_ref, acc):
    slots = arrived_ref.shape[0]
    acc[...] = jnp.zeros_like(acc)

    def step(i, carry):
        tag = tags_ref[i]

        @pl.when(tag >= 0)
        def _():
            lhs = jnp.concatenate([left_ref[0, tag], left_ref[1, tag]], axis=-1)
            acc[tag] += jnp.dot(lhs, arrived_ref[i], preferred_element_type=jnp.float32)

        return carry

    lax.fori_loop(0, slots, step, 0)
    out_ref[...] = acc[...]


SMEM = pl.BlockSpec(memory_space=pltpu.SMEM)
VMEM = pl.BlockSpec(memory_space=pltpu.VMEM)
ANY = pl.BlockSpec(memory_space=pl.ANY)


def full_exchange(psi_blocks, right_ops, slot_source, left_ops, tags):
    terms, sec_dev, width, _ = left_ops.shape
    inter = (
        jnp.einsum("sij,tsjk->stik", psi_blocks, right_ops, preferred_element_type=jnp.float32)
        .astype(jnp.bfloat16)
        .reshape(sec_dev, terms * width, width)
    )
    packed = jnp.take(inter, slot_source, axis=0, mode="clip")
    arrived = lax.all_to_all(packed, "sector", split_axis=0, concat_axis=0, tiled=True)
    partial = pl.pallas_call(
        image_kernel,
        out_shape=jax.ShapeDtypeStruct((sec_dev, width, width), jnp.float32),
        in_specs=[SMEM, VMEM, VMEM],
        out_specs=VMEM,
        scratch_shapes=[pltpu.VMEM((sec_dev, width, width), jnp.float32)],
        compiler_params=pltpu.CompilerParams(vmem_limit_bytes=48 << 20),
        name="images",
    )(tags, left_ops, arrived)
    parts = lax.all_to_all(
        partial.reshape(sec_dev, NX, width // NX, width), "term", split_axis=1, concat_axis=1
    )
    return jnp.sum(parts, axis=1).astype(jnp.bfloat16)


def ring_exchange(order, table, psi_blocks, right_ops, left_ops):
    terms, sec_dev, width, _ = left_ops.shape
    slots = NZ * MEMBERS * CAP
    rows = width // NX
    dma = pltpu.SemaphoreType.DMA
    pieces = sum(range(1, HOPS + 1))

    def blocks(*lead):
        return pltpu.VMEM((*lead, width, width), jnp.bfloat16)

    wave = [blocks(REACH[h]) for h in (0, 1, 2)] * 2 + [blocks(2 * REACH[3])]
    return pl.pallas_call(
        ring_kernel,
        out_shape=(
            jax.ShapeDtypeStruct((slots, rows, width), jnp.float32),
            jax.ShapeDtypeStruct((MEMBERS, NZ, 1, 128), jnp.int32),
        ),
        in_specs=[SMEM, VMEM, ANY, ANY, ANY],
        out_specs=(VMEM, VMEM),
        scratch_shapes=[
            blocks(sec_dev),
            blocks(terms, sec_dev),
            blocks(terms, sec_dev),
            blocks(sec_dev),
            blocks(sec_dev),
            *wave,
            *wave,
            pltpu.VMEM((2, NZ, MEMBERS, CAP * width, width), jnp.bfloat16),
            pltpu.VMEM((2, NZ, MEMBERS, CAP * width, width), jnp.bfloat16),
            pltpu.VMEM((NX - 1, slots, rows, width), jnp.bfloat16),
            pltpu.VMEM((NX - 1, slots, rows, width), jnp.bfloat16),
            pltpu.VMEM((NZ, 1, 128), jnp.int32),
            pltpu.SMEM((NZ, 1, 128), jnp.int32),
            pltpu.VMEM((MEMBERS, NZ, 1, 128), jnp.int32),
            pltpu.SMEM((MEMBERS, NZ, 1, 128), jnp.int32),
            dma((3,)),
            dma((4,)),
            dma((2, 2, pieces)),
            dma((2, 2, pieces)),
            dma((2, NZ, MEMBERS)),
            dma((2, NZ, MEMBERS)),
            dma((NZ, NX)),
            dma((NZ, NX)),
            dma((NZ,)),
            dma((NZ,)),
            dma((MEMBERS,)),
            dma((MEMBERS,)),
        ],
        compiler_params=pltpu.CompilerParams(
            collective_id=0, has_side_effects=True, vmem_limit_bytes=63 << 20
        ),
        name="ring",
    )(order, table, psi_blocks, right_ops, left_ops)


def local(psi_blocks, right_ops, left_ops, owner_map, left_local):
    sec_dev, width, _ = psi_blocks.shape
    slots = lax.axis_size("sector") * CAP
    mine = lax.axis_index("sector")
    my_c, my_z, my_y = mine % NC, (mine // NC) % NZ, mine // (NC * NZ)
    my_member = my_y * NC + my_c
    owners = owner_map[:, 0]
    ranks = ranks_of(owners)
    position, order, fits = plan_of(owners, my_z)
    table = tables_of(owners, ranks, left_local[:, 0], position, fits, my_z)
    found, tables = ring_exchange(order, table, psi_blocks, right_ops, left_ops)
    tables = tables.reshape(MEMBERS * NZ, 1, 128)
    all_fit = jnp.min(tables[:, 0, 127]) > 0

    def by_ring(found, tables, psi_blocks, right_ops, left_ops):
        return pl.pallas_call(
            gather_kernel,
            out_shape=jax.ShapeDtypeStruct((sec_dev, width // NX, width), jnp.bfloat16),
            in_specs=[SMEM, SMEM, VMEM],
            out_specs=VMEM,
            scratch_shapes=[pltpu.VMEM((sec_dev, width // NX, width), jnp.float32)],
            name="gather",
        )(my_member.reshape(1), tables, found)

    def by_all(found, tables, psi_blocks, right_ops, left_ops):
        slot_id = owners * CAP + ranks
        hot = slot_id[None, :] == lax.broadcasted_iota(jnp.int32, (slots, sec_dev), 0)
        slot_source = jnp.sum(
            jnp.where(hot, lax.broadcasted_iota(jnp.int32, (slots, sec_dev), 1), 0), axis=1
        )
        tags = lax.dynamic_slice_in_dim(
            tables[:, 0], (MEMBERS + my_member) * CAP, CAP, axis=1
        ).reshape(NY, NC, NZ, CAP)
        tags = tags.transpose(0, 2, 1, 3).reshape(slots)
        return full_exchange(psi_blocks, right_ops, slot_source, left_ops, tags)

    return lax.cond(
        all_fit, by_ring, by_all, found, tables, psi_blocks, right_ops, left_ops
    )


def solution(mesh):
    placed = (
        P("sector", None, None),
        P("term", "sector", None, None),
        P("term", "sector", None, None),
        P("sector", None),
        P("sector", None),
    )
    return jax.shard_map(
        local, mesh=mesh, in_specs=placed, out_specs=P("sector", "term", None), check_vma=False
    )
```

time: 220 us -> 182 us (0.83)
  Pallas kernels: 187 us -> 164 us
  between operations: 22.9 us -> 9.51 us
  local copies, waits for them, and re-layouts: 4.07 us -> 0.87 us
    pallas_call x3 -> x2, Pallas kernels: 187 us -> 164 us  [the longest x1 159 us: ring_exchange(): pl.pallas_call(ring_kernel, out_shape=(jax.ShapeDtypeStruct((slots, rows,...]
where the time goes in v3:
time: 182 us
  Pallas kernels  164 us (90%)
  between operations  9.51 us (5%)
  other arithmetic  7.03 us (4%)
    pallas_call x1, Pallas kernels, ring_exchange(): pl.pallas_call(ring_kernel, out_shape=(jax.ShapeDtypeStruct((slots, rows,...  159 us
    pallas_call x1, Pallas kernels, by_ring(): pl.pallas_call(gather_kernel, out_shape=jax.ShapeDtypeStruct((sec_dev, wi...  5.18 us

profile of v3, /device:TPU:1, one launch (start us, length us, event | category | flops | bytes accessed | tf_op | source)
XLA Modules:
  0.0 181.7 jit_solution(12366798293915308789)
XLA Ops:
  0.0 0.7 add_bitcast_fusion
  0.7 0.7 fusion.20
  1.3 0.1 select_reduce_fusion.4
  1.5 1.5 fusion.31
  11.8 0.1 pad.2.clone
  11.8 0.8 convert_reduce_fusion
  12.7 0.7 select_reduce_fusion.3.order
  13.4 1.1 select_reduce_fusion.2
  14.5 0.1 fusion.18
  14.5 0.7 add_add_fusion
  15.2 0.0 copy-start.1
  15.2 159.1 %ring.1 = (f32[128,32,128]{2,1,0:T(8,128)}, s32[8,8,1,128]{3,2,1,0:T(1,128)S(1)}) custom-call(s32[64]{0:T(128)} %select_reduce_fusion.3.order, s32[8,1,128]{2,1,0:T(1,128)} %bitcast.42, bf16[64,128,128]{2,1,0:T(8,128)(2,1)} %psi_far.1, bf16[2,64,128,128]{3,2,1,0:T(8,128)(2,1)} %right_far.1, bf16[2,64,128,128]{3,2,1,0:T(8,128)(2,1)} %left_far.1), custom_call_target="tpu_custom_call" | custom-call | tf_op jit(solution)/shard_map/ring/pallas_call | solution.py:444
  174.3 0.7 slice_reduce_fusion
  175.6 0.0 copy-done.1
  175.7 5.2 %conditional.1 = (bf16[64,32,128]{2,1,0:T(8,128)(2,1)S(1)}) conditional(s32[]{:T(128)} %convert_element_type.54, (s32[8,8,1,128]{3,2,1,0:T(1,128)S(1)}, s32[]{:T(128)}, bf16[2,64,128,128]{3,2,1,0:T(8,128)(2,1)}, bf16[64,128,128]{2,1,0:T(8,128)(2,1)}, s32[64]{0:T(128)S(1)}, /*index=5*/s32[64]{0:T(128)S(1)}, ...), branch_computations={%region_14.17_spmd, %region_17.18_spmd} | conditional | flops 539780096 | bytes 73934440 | solution.py:524
  175.7 5.2 %gather.7 = bf16[64,32,128]{2,1,0:T(8,128)(2,1)S(1)} custom-call(s32[1]{0:T(128)} %bitcast.10.me, s32[64,1,128]{2,1,0:T(1,128)S(1)} %bitcast.39, f32[128,32,128]{2,1,0:T(8,128)} %get-tuple-element.37.found), custom_call_target="tpu_custom_call" | custom-call | tf_op jit(solution)/shard_map/cond/branch_1_fun/gather/pallas_call | solution.py:503
  180.9 0.0 copy-start
  180.9 0.8 copy-done
  (9 shorter events, 0.1 us)
Async XLA Ops:
  15.2 160.4 %copy-start.1 = (s32[64,1]{0,1:T(1,128)S(1)}, s32[64,1]{0,1:T(1,128)}, u32[]{:S(2)}) copy-start(s32[64,1]{0,1:T(1,128)} %param.10) | copy-start | bytes 772
  180.9 0.8 copy-start

commit v4 on v3

--- a/solution.py
+++ b/solution.py
@@ -30,66 +30,99 @@
     return jnp.sum((same & earlier).astype(jnp.int32), axis=-2)
 
 
-def plan_of(owners, my_z):
-    count = owners.shape[0]
-    away = lax.rem(lax.rem(owners // NC, NZ) - my_z + NZ, NZ)
-    counts = [jnp.sum((away == d).astype(jnp.int32)) for d in range(NZ)]
+def down_of(row):
+    n = row.shape[1]
+    same = lax.broadcasted_iota(jnp.int32, (n, n), 0) == lax.broadcasted_iota(jnp.int32, (n, n), 1)
+    return jnp.sum(jnp.where(same, row, 0), axis=1, keepdims=True)
+
+
+def across_of(column):
+    n = column.shape[0]
+    same = lax.broadcasted_iota(jnp.int32, (n, n), 0) == lax.broadcasted_iota(jnp.int32, (n, n), 1)
+    return jnp.sum(jnp.where(same, column, 0), axis=0, keepdims=True)
+
+
+def count_down(hits):
+    return jnp.sum(jnp.where(hits, 1, 0), axis=0, keepdims=True)
+
+
+def count_across(hits):
+    return jnp.sum(jnp.where(hits, 1, 0), axis=1, keepdims=True)
+
+
+def plan_of(owners, local, z):
+    n = owners.shape[1]
+    i = lax.broadcasted_iota(jnp.int32, (n, n), 0)
+    j = lax.broadcasted_iota(jnp.int32, (n, n), 1)
+    owners_down = down_of(owners)
+    ranks = count_down((owners_down == owners) & (i < j))
+    away = ((owners // NC) % NZ - z + NZ) % NZ
+    counts = [count_across(away == d) for d in range(NZ)]
     up = [sum(counts[h:HOPS]) for h in range(1, HOPS)] + [0]
     down = [sum(counts[NZ - h] for h in range(k, HOPS)) for k in range(1, HOPS)] + [0]
     room_up = functools.reduce(jnp.minimum, [REACH[h] - up[h] for h in range(HOPS)])
     room_down = functools.reduce(jnp.minimum, [REACH[h] - down[h] for h in range(HOPS)])
-    far_up = jnp.clip(room_up, 0, counts[HOPS])
-    fits = (room_up >= 0) & (room_down >= counts[HOPS] - far_up)
-    opposite = (away == HOPS).astype(jnp.int32)
-    row = lax.broadcasted_iota(jnp.int32, (count, count), 0)
-    col = lax.broadcasted_iota(jnp.int32, (count, count), 1)
-    far_rank = jnp.sum(jnp.where(row < col, opposite[:, None], 0), axis=0)
+    far_up = jnp.minimum(jnp.maximum(room_up, 0), counts[HOPS])
+    fits = jnp.where((room_up >= 0) & (room_down >= counts[HOPS] - far_up), 1, 0)
+    opposite = down_of(jnp.where(away == HOPS, 1, 0))
+    far_rank = jnp.sum(jnp.where(i < j, opposite, 0), axis=0, keepdims=True)
     signed = jnp.where(
         away == HOPS,
         jnp.where(far_rank < far_up, -HOPS, HOPS),
         jnp.where(away < HOPS, -away, NZ - away),
     )
-    key = signed * count + lax.iota(jnp.int32, count)
-    position = jnp.sum((key[:, None] < key[None, :]).astype(jnp.int32), axis=0)
-    order = jnp.sum(jnp.where(position[None, :] == row, col, 0), axis=1)
-    return position, order, fits
-
-
-def tables_of(owners, ranks, left_local, position, fits, my_z):
-    count = owners.shape[0]
-    shape = (NZ, MEMBERS * CAP, count)
-    mate = lax.broadcasted_iota(jnp.int32, shape, 0)
-    member = lax.broadcasted_iota(jnp.int32, shape, 1) // CAP
-    rank = lax.broadcasted_iota(jnp.int32, shape, 1) % CAP
+    key = signed * n + j[:1]
+    position = count_down(down_of(key) < key)
+    position_down = down_of(position)
+    order = jnp.sum(jnp.where(position_down == j, i, 0), axis=0, keepdims=True)
+
+    wide = NZ * MEMBERS * CAP
+    entry = lax.broadcasted_iota(jnp.int32, (1, wide), 1)
+    mate = entry // (MEMBERS * CAP)
+    member = (entry // CAP) % MEMBERS
     goal = ((member // NC) * NZ + mate) * NC + member % NC
-    hits = (owners == goal) & (ranks == rank)
-    ahead = lax.rem(lax.iota(jnp.int32, NZ) - my_z + NZ, NZ)[:, None]
-    start, size = jnp.zeros_like(ahead), jnp.full_like(ahead, count)
+    hits = (owners_down == goal) & (down_of(ranks) == entry % CAP)
+    ahead = (mate - z + NZ) % NZ
+    start, size = jnp.zeros_like(ahead), jnp.full_like(ahead, n)
     for h in range(1, HOPS):
-        start = jnp.where(ahead == NZ - h, count - REACH[h - 1], start)
+        start = jnp.where(ahead == NZ - h, n - REACH[h - 1], start)
         size = jnp.where((ahead == h) | (ahead == NZ - h), REACH[h - 1], size)
     size = jnp.where(ahead == HOPS, 2 * REACH[-1], size)
-    where = jnp.sum(jnp.where(hits, position, 0), axis=2) - start
-    where = jnp.where(
-        (ahead == HOPS) & (where >= REACH[-1]), where - (count - 2 * REACH[-1]), where
-    )
-    where = jnp.clip(where, 0, size - 1)
-    tags = jnp.sum(jnp.where(hits, left_local + 1, 0), axis=2) - 1
-    flag = jnp.broadcast_to(fits.astype(jnp.int32), (NZ, 128 - 2 * MEMBERS * CAP))
-    return jnp.concatenate([where, tags, flag], axis=1).reshape(NZ, 1, 128)
+    where = jnp.sum(jnp.where(hits, position_down, 0), axis=0, keepdims=True) - start
+    where = jnp.where((ahead == HOPS) & (where >= REACH[-1]), where - (n - 2 * REACH[-1]), where)
+    where = jnp.minimum(jnp.maximum(where, 0), size - 1)
+    tags = jnp.sum(jnp.where(hits, down_of(local) + 1, 0), axis=0, keepdims=True) - 1
+    return order, where, tags, jnp.broadcast_to(fits, (1, wide))
+
+
+def sort_of(tags, slots):
+    n = tags.shape[0]
+    place = lax.broadcasted_iota(jnp.int32, (n, n), 1)
+    tags = jnp.where(tags < 0, n // CAP, tags)
+    key = tags * n + lax.broadcasted_iota(jnp.int32, (n, 1), 0)
+    earlier = across_of(key) < key
+    at = count_across(earlier)
+    follows = jnp.where(count_across(earlier & (across_of(tags) == tags)) > 0, 1, 0)
+    order = jnp.sum(jnp.where(at == place, slots, 0), axis=0, keepdims=True)
+    keep = jnp.sum(jnp.where(at == place, follows, 0), axis=0, keepdims=True)
+    last = jnp.maximum(count_down(tags <= place) - 1, 0)
+    has = jnp.where(count_down(tags == place) > 0, 1, 0)
+    return order, keep, last, has
 
 
 def ring_kernel(
-    order, table, psi_far, right_far, left_far, out, all_tables,
+    owners, local, psi_far, right_far, left_far, out, fit,
     psi, right, left, inter0, inter1,
     up10, up20, up30, down10, down20, down30, far0,
     up11, up21, up31, down11, down21, down31, far1,
-    outgoing, arrived, shares, taken, mates, picks, rowmates, tags,
+    outgoing, arrived, shares, taken, own, runs,
+    order_row, order, table, mates, picks, rowmates, tags, line_rows, lines,
     load, local_sem, ring_send, ring_recv, row_send, row_recv, term_send, term_recv,
     mate_send, mate_recv, table_send, table_recv,
 ):
     count, width = psi.shape[0], psi.shape[1]
     rows = out.shape[1]
+    slots = own.shape[0]
     per_source = MEMBERS * CAP
     x = lax.axis_index("term")
     place = lax.axis_index("sector")
@@ -112,8 +145,6 @@
     ]
     for copy in loads:
         copy.start()
-    own_row = pltpu.make_async_copy(table.at[z], mates.at[z], local_sem.at[0])
-    own_row.start()
     barrier = pltpu.get_barrier_semaphore()
     for d in range(1, NZ):
         pl.semaphore_signal(
@@ -179,7 +210,7 @@
     def mate_copy(d):
         mate = (z + d) % NZ
         return pltpu.make_async_remote_copy(
-            src_ref=table.at[mate],
+            src_ref=table,
             dst_ref=mates.at[z],
             send_sem=mate_send.at[d],
             recv_sem=mate_recv.at[d],
@@ -199,7 +230,7 @@
         )
 
     def multiply(p, carry):
-        s = order[p]
+        s = order[0, p]
         both = jnp.concatenate([right[0, s], right[1, s]], axis=-1)
         made = jnp.dot(psi[s], both, preferred_element_type=jnp.float32).astype(inter0.dtype)
         inter0[p] = made[:, :width]
@@ -211,16 +242,16 @@
 
         def one(j, carry):
             yy, cc = member_of(j)
-            entry = (yy * NC + cc) * CAP
-            outgoing[w, d, j, :width] = held[picks[source, 0, entry]]
-            outgoing[w, d, j, width:] = held[picks[source, 0, entry + 1]]
+            entry = (z * MEMBERS + yy * NC + cc) * CAP
+            outgoing[w, d, j, :width] = held[picks[source, 0, 0, entry]]
+            outgoing[w, d, j, width:] = held[picks[source, 0, 0, entry + 1]]
             row_copy(w, d, j).start()
             return carry
 
         lax.fori_loop(1, MEMBERS, one, 0)
-        entry = my_member * CAP
-        arrived[w, source, my_member, :width] = held[picks[source, 0, entry]]
-        arrived[w, source, my_member, width:] = held[picks[source, 0, entry + 1]]
+        entry = (z * MEMBERS + my_member) * CAP
+        arrived[w, source, my_member, :width] = held[picks[source, 0, 0, entry]]
+        arrived[w, source, my_member, width:] = held[picks[source, 0, 0, entry + 1]]
 
     def images(d):
         source = (z + NZ - d) % NZ
@@ -235,7 +266,7 @@
         def one(m, carry):
             for r in range(CAP):
                 slot = source * per_source + m * CAP + r
-                tag = jnp.maximum(tags[m, source, 0, per_source + my_member * CAP + r], 0)
+                tag = jnp.maximum(tags[m, source, 0, 0, (z * MEMBERS + my_member) * CAP + r], 0)
                 lhs = jnp.concatenate(
                     [
                         jnp.concatenate(
@@ -250,7 +281,7 @@
                     [arrived[t, source, m, r * width : (r + 1) * width] for t in range(2)], axis=0
                 )
                 image = jnp.dot(lhs, rhs, preferred_element_type=jnp.float32)
-                out[slot] = image[:rows]
+                own[slot] = image[:rows]
                 for dx in range(1, NX):
                     shares[dx - 1, slot] = image[dx * rows : (dx + 1) * rows].astype(shares.dtype)
             return carry
@@ -259,6 +290,13 @@
         for dx in range(1, NX):
             term_copy(d, dx).start()
 
+    plan = plan_of(owners[...], local[...], z)
+    order_row[:, :count] = plan[0]
+    to_order = pltpu.make_async_copy(order_row, order, local_sem.at[0])
+    to_order.start()
+    for k in range(3):
+        table[k] = plan[k + 1]
+    to_order.wait()
     loads[0].wait()
     loads[1].wait()
     edges = [0, *reversed(REACH)]
@@ -276,26 +314,45 @@
         ring_copy(0, 0, 1, k).start()
         ring_copy(0, 1, 1, k).start()
 
-    own_row.wait()
+    own_table = pltpu.make_async_copy(table, mates.at[z], local_sem.at[1])
+    own_table.start()
+    own_table.wait()
     for d in range(1, NZ):
         mate_copy(d).wait_recv()
     for j in range(1, MEMBERS):
         table_copy(j).start()
-    to_picks = pltpu.make_async_copy(mates, picks, local_sem.at[1])
+    to_picks = pltpu.make_async_copy(mates, picks, local_sem.at[2])
     to_picks.start()
-    own_rows = pltpu.make_async_copy(mates, rowmates.at[my_member], local_sem.at[2])
-    own_rows.start()
+    own_tables = pltpu.make_async_copy(mates, rowmates.at[my_member], local_sem.at[3])
+    own_tables.start()
     to_picks.wait()
     for w in range(2):
         hand_on(w, 0, inter[w])
-    own_rows.wait()
+    own_tables.wait()
     for j in range(1, MEMBERS):
         table_copy(j).wait_recv()
-    to_tags = pltpu.make_async_copy(rowmates, tags, local_sem.at[3])
+    to_tags = pltpu.make_async_copy(rowmates.at[:, :, pl.ds(1, 1)], tags, local_sem.at[4])
     to_tags.start()
+    every = jnp.min(rowmates[:, :, 2, 0], axis=0)
+    fit[...] = jnp.broadcast_to(jnp.min(every, axis=0, keepdims=True), fit.shape)
+    lane = lax.broadcasted_iota(jnp.int32, (1, 1, slots), 2)
+    known = rowmates[:, :, 1, 0]
+    mine = [
+        jnp.sum(
+            jnp.where(lane == (z * MEMBERS + my_member) * CAP + r, known, 0), axis=2, keepdims=True
+        ).reshape(MEMBERS * NZ, 1)
+        for r in range(CAP)
+    ]
+    row = lax.broadcasted_iota(jnp.int32, (slots, 1), 0)
+    source_of, member_at = row % NZ, (row // NZ) % MEMBERS
+    slot_at = source_of * per_source + member_at * CAP + row // (MEMBERS * NZ)
+    line = sort_of(jnp.concatenate(mine, axis=0), slot_at)
+    for k in range(4):
+        line_rows[k] = line[k]
+    to_lines = pltpu.make_async_copy(line_rows, lines, local_sem.at[5])
+    to_lines.start()
     to_tags.wait()
-    for m in range(MEMBERS):
-        all_tables[m] = rowmates[m]
+    to_lines.wait()
     loads[2].wait()
 
     waiting = [0]
@@ -336,15 +393,25 @@
 
     lax.fori_loop(0, NZ, settle, 0)
 
-    def total(slot, carry):
-        out[slot] = out[slot] + (
+    def total(p, run):
+        slot = lines[0, 0, p]
+        found = own[slot] + (
             taken[0, slot].astype(jnp.float32)
             + taken[1, slot].astype(jnp.float32)
             + taken[2, slot].astype(jnp.float32)
         )
+        run = found + lines[1, 0, p].astype(jnp.float32) * run
+        runs[p] = run
+        return run
+
+    lax.fori_loop(0, slots, total, jnp.zeros(own.shape[1:], jnp.float32), unroll=4)
+
+    def give(l, carry):
+        kept = lines[3, 0, l].astype(jnp.float32)
+        out[l] = (kept * runs[lines[2, 0, l]]).astype(out.dtype)
         return carry
 
-    lax.fori_loop(0, out.shape[0], total, 0, unroll=4)
+    lax.fori_loop(0, out.shape[0], give, 0, unroll=4)
 
     for w in range(2):
         for way in range(2):
@@ -364,23 +431,6 @@
         return carry
 
     lax.fori_loop(0, NZ, sent, 0)
-
-
-def gather_kernel(me, tables, found, out, acc):
-    acc[...] = jnp.zeros_like(acc)
-    column = (MEMBERS + me[0]) * CAP
-
-    def step(i, carry):
-        tag = tables[((i // CAP) % MEMBERS) * NZ + i // (MEMBERS * CAP), 0, column + i % CAP]
-
-        @pl.when(tag >= 0)
-        def _():
-            acc[tag] += found[i]
-
-        return carry
-
-    lax.fori_loop(0, found.shape[0], step, 0)
-    out[...] = acc[...].astype(out.dtype)
 
 
 def image_kernel(tags_ref, left_ref, arrived_ref, out_ref, acc):
@@ -430,7 +480,7 @@
     return jnp.sum(parts, axis=1).astype(jnp.bfloat16)
 
 
-def ring_exchange(order, table, psi_blocks, right_ops, left_ops):
+def ring_exchange(owners, local, psi_blocks, right_ops, left_ops):
     terms, sec_dev, width, _ = left_ops.shape
     slots = NZ * MEMBERS * CAP
     rows = width // NX
@@ -444,10 +494,10 @@
     return pl.pallas_call(
         ring_kernel,
         out_shape=(
-            jax.ShapeDtypeStruct((slots, rows, width), jnp.float32),
-            jax.ShapeDtypeStruct((MEMBERS, NZ, 1, 128), jnp.int32),
+            jax.ShapeDtypeStruct((sec_dev, rows, width), jnp.bfloat16),
+            jax.ShapeDtypeStruct((8, slots), jnp.int32),
         ),
-        in_specs=[SMEM, VMEM, ANY, ANY, ANY],
+        in_specs=[VMEM, VMEM, ANY, ANY, ANY],
         out_specs=(VMEM, VMEM),
         scratch_shapes=[
             blocks(sec_dev),
@@ -461,12 +511,19 @@
             pltpu.VMEM((2, NZ, MEMBERS, CAP * width, width), jnp.bfloat16),
             pltpu.VMEM((NX - 1, slots, rows, width), jnp.bfloat16),
             pltpu.VMEM((NX - 1, slots, rows, width), jnp.bfloat16),
-            pltpu.VMEM((NZ, 1, 128), jnp.int32),
-            pltpu.SMEM((NZ, 1, 128), jnp.int32),
-            pltpu.VMEM((MEMBERS, NZ, 1, 128), jnp.int32),
-            pltpu.SMEM((MEMBERS, NZ, 1, 128), jnp.int32),
+            pltpu.VMEM((slots, rows, width), jnp.float32),
+            pltpu.VMEM((slots, rows, width), jnp.float32),
+            pltpu.VMEM((1, slots), jnp.int32),
+            pltpu.SMEM((1, slots), jnp.int32),
+            pltpu.VMEM((3, 1, slots), jnp.int32),
+            pltpu.VMEM((NZ, 3, 1, slots), jnp.int32),
+            pltpu.SMEM((NZ, 3, 1, slots), jnp.int32),
+            pltpu.VMEM((MEMBERS, NZ, 3, 1, slots), jnp.int32),
+            pltpu.SMEM((MEMBERS, NZ, 1, 1, slots), jnp.int32),
+            pltpu.VMEM((4, 1, slots), jnp.int32),
+            pltpu.SMEM((4, 1, slots), jnp.int32),
             dma((3,)),
-            dma((4,)),
+            dma((6,)),
             dma((2, 2, pieces)),
             dma((2, 2, pieces)),
             dma((2, NZ, MEMBERS)),
@@ -482,47 +539,35 @@
             collective_id=0, has_side_effects=True, vmem_limit_bytes=63 << 20
         ),
         name="ring",
-    )(order, table, psi_blocks, right_ops, left_ops)
+    )(owners, local, psi_blocks, right_ops, left_ops)
 
 
 def local(psi_blocks, right_ops, left_ops, owner_map, left_local):
     sec_dev, width, _ = psi_blocks.shape
-    slots = lax.axis_size("sector") * CAP
-    mine = lax.axis_index("sector")
-    my_c, my_z, my_y = mine % NC, (mine // NC) % NZ, mine // (NC * NZ)
-    my_member = my_y * NC + my_c
-    owners = owner_map[:, 0]
-    ranks = ranks_of(owners)
-    position, order, fits = plan_of(owners, my_z)
-    table = tables_of(owners, ranks, left_local[:, 0], position, fits, my_z)
-    found, tables = ring_exchange(order, table, psi_blocks, right_ops, left_ops)
-    tables = tables.reshape(MEMBERS * NZ, 1, 128)
-    all_fit = jnp.min(tables[:, 0, 127]) > 0
-
-    def by_ring(found, tables, psi_blocks, right_ops, left_ops):
-        return pl.pallas_call(
-            gather_kernel,
-            out_shape=jax.ShapeDtypeStruct((sec_dev, width // NX, width), jnp.bfloat16),
-            in_specs=[SMEM, SMEM, VMEM],
-            out_specs=VMEM,
-            scratch_shapes=[pltpu.VMEM((sec_dev, width // NX, width), jnp.float32)],
-            name="gather",
-        )(my_member.reshape(1), tables, found)
-
-    def by_all(found, tables, psi_blocks, right_ops, left_ops):
-        slot_id = owners * CAP + ranks
+    n_sector = lax.axis_size("sector")
+    slots = n_sector * CAP
+    found, fit = ring_exchange(
+        owner_map.reshape(1, sec_dev), left_local.reshape(1, sec_dev), psi_blocks, right_ops, left_ops
+    )
+
+    def by_ring(found, psi_blocks, right_ops, left_ops, owner_map, left_local):
+        return found
+
+    def by_all(found, psi_blocks, right_ops, left_ops, owner_map, left_local):
+        owners = owner_map[:, 0]
+        slot_id = owners * CAP + ranks_of(owners)
         hot = slot_id[None, :] == lax.broadcasted_iota(jnp.int32, (slots, sec_dev), 0)
         slot_source = jnp.sum(
             jnp.where(hot, lax.broadcasted_iota(jnp.int32, (slots, sec_dev), 1), 0), axis=1
         )
-        tags = lax.dynamic_slice_in_dim(
-            tables[:, 0], (MEMBERS + my_member) * CAP, CAP, axis=1
-        ).reshape(NY, NC, NZ, CAP)
-        tags = tags.transpose(0, 2, 1, 3).reshape(slots)
+        own_tags = jnp.max(jnp.where(hot, left_local[:, 0][None, :], -1), axis=1)
+        tags = lax.all_to_all(
+            own_tags.reshape(n_sector, CAP), "sector", split_axis=0, concat_axis=0, tiled=True
+        ).reshape(slots)
         return full_exchange(psi_blocks, right_ops, slot_source, left_ops, tags)
 
     return lax.cond(
-        all_fit, by_ring, by_all, found, tables, psi_blocks, right_ops, left_ops
+        fit[0, 0] > 0, by_ring, by_all, found, psi_blocks, right_ops, left_ops, owner_map, left_local
     )
 
 

time: 182 us -> 162 us (0.89)
  between operations: 9.51 us -> 0.69 us
  other arithmetic: 7.03 us -> 0 us
  Pallas kernels: 164 us -> 159 us
    pallas_call x2 -> x1, Pallas kernels: 164 us -> 159 us  [ring_exchange(): pl.pallas_call(ring_kernel, out_shape=(jax.ShapeDtypeStruct((sec_dev, row...]
    reduce_sum x5 -> x0, other arithmetic: 4.17 us -> none  [the longest x1 1.45 us: plan_of(): counts = [jnp.sum((away == d).astype(jnp.int32)) for d in range(NZ)]]
where the time goes in v4:
time: 162 us
  Pallas kernels  159 us (98%)
  local copies, waits for them, and re-layouts  2 us (1%)
    pallas_call x1, Pallas kernels, ring_exchange(): pl.pallas_call(ring_kernel, out_shape=(jax.ShapeDtypeStruct((sec_dev, row...  159 us

profile of v4, /device:TPU:1, one launch (start us, length us, event | category | flops | bytes accessed | tf_op | source)
XLA Modules:
  0.0 161.6 jit_solution(3428381874464790385)
XLA Ops:
  0.0 0.0 copy-start
  0.0 0.0 copy-start.1
  0.0 158.9 %ring.1 = (bf16[64,32,128]{2,1,0:T(8,128)(2,1)S(1)}, s32[8,128]{1,0:T(8,128)}) custom-call(s32[1,64]{1,0:T(1,128)} %bitcast.20, s32[1,64]{1,0:T(1,128)} %bitcast.18, bf16[64,128,128]{2,1,0:T(8,128)(2,1)} %psi_far.1, bf16[2,64,128,128]{3,2,1,0:T(8,128)(2,1)} %right_far.1, bf16[2,64,128,128]{3,2,1,0:T(8,128)(2,1)} %left_far.1), custom_call_target="tpu_custom_call" | custom-call | tf_op jit(solution)/shard_map/ring/pallas_call | solution.py:494
  158.9 1.2 slice.3
  160.7 0.0 copy-done
  160.7 0.0 copy-done.1
  160.8 0.8 copy.24
  (1 shorter events, 0.0 us)
Async XLA Ops:
  0.0 160.7 %copy-start = (s32[64,1]{0,1:T(1,128)S(1)}, s32[64,1]{0,1:T(1,128)}, u32[]{:S(2)}) copy-start(s32[64,1]{0,1:T(1,128)} %param.11) | copy-start | bytes 772
  0.0 160.7 %copy-start.1 = (s32[64,1]{0,1:T(1,128)S(1)}, s32[64,1]{0,1:T(1,128)}, u32[]{:S(2)}) copy-start(s32[64,1]{0,1:T(1,128)} %param.10) | copy-start | bytes 772

commit v5 on v4

--- a/solution.py
+++ b/solution.py
@@ -286,7 +286,7 @@
                     shares[dx - 1, slot] = image[dx * rows : (dx + 1) * rows].astype(shares.dtype)
             return carry
 
-        lax.fori_loop(0, MEMBERS, one, 0)
+        lax.fori_loop(0, MEMBERS, one, 0, unroll=4)
         for dx in range(1, NX):
             term_copy(d, dx).start()
 
@@ -334,7 +334,7 @@
     to_tags = pltpu.make_async_copy(rowmates.at[:, :, pl.ds(1, 1)], tags, local_sem.at[4])
     to_tags.start()
     every = jnp.min(rowmates[:, :, 2, 0], axis=0)
-    fit[...] = jnp.broadcast_to(jnp.min(every, axis=0, keepdims=True), fit.shape)
+    line_rows[4] = jnp.min(every, axis=0, keepdims=True)
     lane = lax.broadcasted_iota(jnp.int32, (1, 1, slots), 2)
     known = rowmates[:, :, 1, 0]
     mine = [
@@ -353,9 +353,10 @@
     to_lines.start()
     to_tags.wait()
     to_lines.wait()
+    fit[0] = lines[4, 0, 0]
     loads[2].wait()
 
-    waiting = [0]
+    early = {(0, 2, 0): [0], (1, 2, 0): [1], (1, 2, 1): [NZ - 1], (1, 3, 0): [2], (1, 4, 0): [NZ - 2]}
     for w in range(2):
         for hop in range(1, HOPS + 1):
             pieces = len(chunk_bounds(hop))
@@ -373,45 +374,49 @@
                     if between:
                         ring_copy(1, 0, 1, HOPS - 1).start()
                         ring_copy(1, 1, 1, HOPS - 1).start()
+                    for d in early.get((w, hop, k), ()):
+                        images(d)
+            hand_on(w, hop, up[w][hop])
             if hop < HOPS:
-                hand_on(w, hop, up[w][hop])
                 hand_on(w, NZ - hop, down[w][hop])
-                arriving = [hop, NZ - hop]
-            else:
-                hand_on(w, hop, up[w][hop])
-                arriving = [hop]
-            for d in waiting:
-                images(d)
-            waiting = arriving if w == 1 else []
-    for d in waiting:
+            if k == pieces - 1:
+                for d in early.get((w, hop, k), ()):
+                    images(d)
+    for d in (HOPS - 1, NZ - HOPS + 1, HOPS):
         images(d)
 
-    def settle(d, carry):
+    def settle(d):
         for dx in range(1, NX):
             term_copy(d, dx).wait_recv()
-        return carry
-
-    lax.fori_loop(0, NZ, settle, 0)
+        first = ((z + NZ - d) % NZ) * per_source
+
+        def add(i, carry):
+            slot = first + i
+            own[slot] += (
+                taken[0, slot].astype(jnp.float32)
+                + taken[1, slot].astype(jnp.float32)
+                + taken[2, slot].astype(jnp.float32)
+            )
+            return carry
+
+        lax.fori_loop(0, per_source, add, 0, unroll=4)
+
+    for d in (0, 1, NZ - 1, 2, NZ - 2, HOPS - 1, NZ - HOPS + 1, HOPS):
+        settle(d)
 
     def total(p, run):
-        slot = lines[0, 0, p]
-        found = own[slot] + (
-            taken[0, slot].astype(jnp.float32)
-            + taken[1, slot].astype(jnp.float32)
-            + taken[2, slot].astype(jnp.float32)
-        )
-        run = found + lines[1, 0, p].astype(jnp.float32) * run
+        run = own[lines[0, 0, p]] + lines[1, 0, p].astype(jnp.float32) * run
         runs[p] = run
         return run
 
-    lax.fori_loop(0, slots, total, jnp.zeros(own.shape[1:], jnp.float32), unroll=4)
+    lax.fori_loop(0, slots, total, jnp.zeros(own.shape[1:], jnp.float32), unroll=8)
 
     def give(l, carry):
         kept = lines[3, 0, l].astype(jnp.float32)
         out[l] = (kept * runs[lines[2, 0, l]]).astype(out.dtype)
         return carry
 
-    lax.fori_loop(0, out.shape[0], give, 0, unroll=4)
+    lax.fori_loop(0, out.shape[0], give, 0, unroll=8)
 
     for w in range(2):
         for way in range(2):
@@ -495,10 +500,10 @@
         ring_kernel,
         out_shape=(
             jax.ShapeDtypeStruct((sec_dev, rows, width), jnp.bfloat16),
-            jax.ShapeDtypeStruct((8, slots), jnp.int32),
+            jax.ShapeDtypeStruct((1,), jnp.int32),
         ),
         in_specs=[VMEM, VMEM, ANY, ANY, ANY],
-        out_specs=(VMEM, VMEM),
+        out_specs=(VMEM, SMEM),
         scratch_shapes=[
             blocks(sec_dev),
             blocks(terms, sec_dev),
@@ -520,8 +525,8 @@
             pltpu.SMEM((NZ, 3, 1, slots), jnp.int32),
             pltpu.VMEM((MEMBERS, NZ, 3, 1, slots), jnp.int32),
             pltpu.SMEM((MEMBERS, NZ, 1, 1, slots), jnp.int32),
-            pltpu.VMEM((4, 1, slots), jnp.int32),
-            pltpu.SMEM((4, 1, slots), jnp.int32),
+            pltpu.VMEM((5, 1, slots), jnp.int32),
+            pltpu.SMEM((5, 1, slots), jnp.int32),
             dma((3,)),
             dma((6,)),
             dma((2, 2, pieces)),
@@ -567,7 +572,7 @@
         return full_exchange(psi_blocks, right_ops, slot_source, left_ops, tags)
 
     return lax.cond(
-        fit[0, 0] > 0, by_ring, by_all, found, psi_blocks, right_ops, left_ops, owner_map, left_local
+        fit[0] > 0, by_ring, by_all, found, psi_blocks, right_ops, left_ops, owner_map, left_local
     )
 
 

time: 162 us -> 158 us (0.975)
  Pallas kernels: 159 us -> 157 us
    pallas_call x1, Pallas kernels: 159 us -> 157 us  [ring_exchange(): pl.pallas_call(ring_kernel, out_shape=(jax.ShapeDtypeStruct((sec_dev, row...]
where the time goes in v5:
time: 158 us
  Pallas kernels  157 us (99%)
    pallas_call x1, Pallas kernels, ring_exchange(): pl.pallas_call(ring_kernel, out_shape=(jax.ShapeDtypeStruct((sec_dev, row...  157 us

profile of v5, /device:TPU:1, one launch (start us, length us, event | category | flops | bytes accessed | tf_op | source)
XLA Modules:
  0.0 158.1 jit_solution(8447467300276737091)
XLA Ops:
  0.0 0.0 copy-start
  0.0 0.0 copy-start.1
  0.0 156.6 %ring.1 = (bf16[64,32,128]{2,1,0:T(8,128)(2,1)S(1)}, s32[1]{0:T(128)}) custom-call(s32[1,64]{1,0:T(1,128)} %bitcast.20, s32[1,64]{1,0:T(1,128)} %bitcast.18, bf16[64,128,128]{2,1,0:T(8,128)(2,1)} %psi_far.1, bf16[2,64,128,128]{3,2,1,0:T(8,128)(2,1)} %right_far.1, bf16[2,64,128,128]{3,2,1,0:T(8,128)(2,1)} %left_far.1), custom_call_target="tpu_custom_call" | custom-call | tf_op jit(solution)/shard_map/ring/pallas_call | solution.py:499
  157.3 0.0 copy-done
  157.3 0.0 copy-done.1
  157.3 0.8 copy.24
  (1 shorter events, 0.0 us)
Async XLA Ops:
  0.0 157.3 %copy-start = (s32[64,1]{0,1:T(1,128)S(1)}, s32[64,1]{0,1:T(1,128)}, u32[]{:S(2)}) copy-start(s32[64,1]{0,1:T(1,128)} %param.11) | copy-start | bytes 772
  0.0 157.3 %copy-start.1 = (s32[64,1]{0,1:T(1,128)S(1)}, s32[64,1]{0,1:T(1,128)}, u32[]{:S(2)}) copy-start(s32[64,1]{0,1:T(1,128)} %param.10) | copy-start | bytes 772

commit v6 on v5

--- a/solution.py
+++ b/solution.py
@@ -14,6 +14,8 @@
 MEMBERS = NY * NC
 REACH = (33, 24, 16, 7)
 HOPS = len(REACH)
+WAVES = 3
+HALVES = ((0,), (1, 2))
 
 
 def chunk_bounds(hop):
@@ -110,19 +112,29 @@
     return order, keep, last, has
 
 
-def ring_kernel(
-    owners, local, psi_far, right_far, left_far, out, fit,
-    psi, right, left, inter0, inter1,
-    up10, up20, up30, down10, down20, down30, far0,
-    up11, up21, up31, down11, down21, down31, far1,
-    outgoing, arrived, shares, taken, own, runs,
-    order_row, order, table, mates, picks, rowmates, tags, line_rows, lines,
-    load, local_sem, ring_send, ring_recv, row_send, row_recv, term_send, term_recv,
-    mate_send, mate_recv, table_send, table_recv,
-):
+def ring_kernel(owners, local, psi_far, right_far, left_far, out, fit, psi, right, left, *refs):
+    refs = list(refs)
+
+    def take(number):
+        taken_refs = refs[:number]
+        del refs[:number]
+        return taken_refs
+
+    inter = take(WAVES)
+    up, down = [], []
+    for w in range(WAVES):
+        up1, up2, up3, down1, down2, down3, far = take(7)
+        up.append((inter[w], up1, up2, up3, far))
+        down.append((inter[w], down1, down2, down3, far))
+    outgoing, arrived = take(WAVES), take(WAVES)
+    shares, taken, own, full, runs = take(5)
+    order_row, order, table, mates, picks, rowmates, tags, line_rows, lines = take(9)
+    load, local_sem, ring_send, ring_recv, row_send, row_recv, term_send, term_recv = take(8)
+    mate_send, mate_recv, table_send, table_recv = take(4)
     count, width = psi.shape[0], psi.shape[1]
     rows = out.shape[1]
-    slots = own.shape[0]
+    slots = full.shape[0]
+    half = width // 2
     per_source = MEMBERS * CAP
     x = lax.axis_index("term")
     place = lax.axis_index("sector")
@@ -156,9 +168,6 @@
     for d in range(1, NX):
         pl.semaphore_signal(barrier, inc=1, device_id={"term": (x + d) % NX}, device_id_type=MESH)
 
-    inter = (inter0, inter1)
-    up = ((inter0, up10, up20, up30, far0), (inter1, up11, up21, up31, far1))
-    down = ((inter0, down10, down20, down30, far0), (inter1, down11, down21, down31, far1))
     reach_far = REACH[-1]
     number = {}
     for hop in range(1, HOPS + 1):
@@ -188,21 +197,21 @@
     def row_copy(w, d, j):
         yy, cc = member_of(j)
         return pltpu.make_async_remote_copy(
-            src_ref=outgoing.at[w, d, j],
-            dst_ref=arrived.at[w, (z + NZ - d) % NZ, my_member],
+            src_ref=outgoing[w].at[d, j],
+            dst_ref=arrived[w].at[(z + NZ - d) % NZ, my_member],
             send_sem=row_send.at[w, d, j],
             recv_sem=row_recv.at[w, d, j],
             device_id=sector_id(yy, z, cc),
             device_id_type=MESH,
         )
 
-    def term_copy(d, dx):
-        group = pl.ds(((z + NZ - d) % NZ) * per_source, per_source)
+    def term_copy(h, d, dx):
+        group = pl.ds(((z + NZ - d) % NZ) * MEMBERS, MEMBERS)
         return pltpu.make_async_remote_copy(
-            src_ref=shares.at[dx - 1, group],
-            dst_ref=taken.at[dx - 1, group],
-            send_sem=term_send.at[d, dx],
-            recv_sem=term_recv.at[d, dx],
+            src_ref=shares.at[h, dx - 1, group],
+            dst_ref=taken.at[h, dx - 1, group],
+            send_sem=term_send.at[h, d, dx],
+            recv_sem=term_recv.at[h, d, dx],
             device_id={"term": (x + dx) % NX},
             device_id_type=MESH,
         )
@@ -229,66 +238,81 @@
             device_id_type=MESH,
         )
 
+    low = lax.broadcasted_iota(jnp.int32, (width, width), 1) < half
+    low_rows = lax.broadcasted_iota(jnp.int32, (rows, width), 1) < half
+
+    def turned(value):
+        return pltpu.roll(value, half, 1)
+
     def multiply(p, carry):
         s = order[0, p]
         both = jnp.concatenate([right[0, s], right[1, s]], axis=-1)
-        made = jnp.dot(psi[s], both, preferred_element_type=jnp.float32).astype(inter0.dtype)
-        inter0[p] = made[:, :width]
-        inter1[p] = made[:, width:]
+        made = jnp.dot(psi[s], both, preferred_element_type=jnp.float32)
+        one, two = made[:, :width], made[:, width:]
+        inter[0][p] = jnp.where(low, one, turned(two)).astype(jnp.bfloat16)
+        late = jnp.where(low, turned(one), two).astype(jnp.bfloat16)
+        inter[1][p] = late[:half]
+        inter[2][p] = late[half:]
         return carry
 
     def hand_on(w, d, held):
         source = (z + NZ - d) % NZ
+        tall = held.shape[1]
 
         def one(j, carry):
             yy, cc = member_of(j)
             entry = (z * MEMBERS + yy * NC + cc) * CAP
-            outgoing[w, d, j, :width] = held[picks[source, 0, 0, entry]]
-            outgoing[w, d, j, width:] = held[picks[source, 0, 0, entry + 1]]
+            outgoing[w][d, j, :tall] = held[picks[source, 0, 0, entry]]
+            outgoing[w][d, j, tall:] = held[picks[source, 0, 0, entry + 1]]
             row_copy(w, d, j).start()
             return carry
 
         lax.fori_loop(1, MEMBERS, one, 0)
         entry = (z * MEMBERS + my_member) * CAP
-        arrived[w, source, my_member, :width] = held[picks[source, 0, 0, entry]]
-        arrived[w, source, my_member, width:] = held[picks[source, 0, 0, entry + 1]]
-
-    def images(d):
+        arrived[w][source, my_member, :tall] = held[picks[source, 0, 0, entry]]
+        arrived[w][source, my_member, tall:] = held[picks[source, 0, 0, entry + 1]]
+
+    def images(h, d):
         source = (z + NZ - d) % NZ
 
         def landed(j, carry):
-            row_copy(0, d, j).wait_recv()
-            row_copy(1, d, j).wait_recv()
+            for w in HALVES[h]:
+                row_copy(w, d, j).wait_recv()
             return carry
 
         lax.fori_loop(1, MEMBERS, landed, 0)
 
         def one(m, carry):
+            made = []
             for r in range(CAP):
-                slot = source * per_source + m * CAP + r
                 tag = jnp.maximum(tags[m, source, 0, 0, (z * MEMBERS + my_member) * CAP + r], 0)
                 lhs = jnp.concatenate(
                     [
-                        jnp.concatenate(
-                            [left[t, tag, pl.ds(((x + dx) % NX) * rows, rows)] for dx in range(NX)],
-                            axis=0,
-                        )
+                        left[t, tag, pl.ds(((x + dx) % NX) * rows, rows)]
                         for t in range(2)
+                        for dx in range(NX)
                     ],
-                    axis=1,
+                    axis=0,
                 )
-                rhs = jnp.concatenate(
-                    [arrived[t, source, m, r * width : (r + 1) * width] for t in range(2)], axis=0
-                )
-                image = jnp.dot(lhs, rhs, preferred_element_type=jnp.float32)
-                own[slot] = image[:rows]
-                for dx in range(1, NX):
-                    shares[dx - 1, slot] = image[dx * rows : (dx + 1) * rows].astype(shares.dtype)
+                pieces = []
+                for w in HALVES[h]:
+                    tall = inter[w].shape[1]
+                    pieces.append(arrived[w][source, m, r * tall : (r + 1) * tall])
+                rhs = pieces[0] if len(pieces) == 1 else jnp.concatenate(pieces, axis=0)
+                both = jnp.dot(lhs, rhs, preferred_element_type=jnp.float32)
+                made.append((both[:width], both[width:]))
+            pair = jnp.where(
+                low, made[0][0] + turned(made[0][1]), turned(made[1][0]) + made[1][1]
+            )
+            at = source * MEMBERS + m
+            own[h, at] = pair[:rows]
+            for dx in range(1, NX):
+                shares[h, dx - 1, at] = pair[dx * rows : (dx + 1) * rows].astype(shares.dtype)
             return carry
 
-        lax.fori_loop(0, MEMBERS, one, 0, unroll=4)
+        lax.fori_loop(0, MEMBERS, one, 0, unroll=2)
         for dx in range(1, NX):
-            term_copy(d, dx).start()
+            term_copy(h, d, dx).start()
 
     plan = plan_of(owners[...], local[...], z)
     order_row[:, :count] = plan[0]
@@ -305,8 +329,8 @@
     ]
     spans[-1] = [(edges[HOPS - 1], count - edges[HOPS - 1])]
     for k in range(HOPS):
-        for low, high in spans[k]:
-            lax.fori_loop(low, high, multiply, 0, unroll=True)
+        for begin, end in spans[k]:
+            lax.fori_loop(begin, end, multiply, 0, unroll=True)
         if k == 0:
             pl.semaphore_wait(barrier, NZ - 1 + MEMBERS - 1 + NX - 1)
             for d in range(1, NZ):
@@ -326,7 +350,7 @@
     own_tables = pltpu.make_async_copy(mates, rowmates.at[my_member], local_sem.at[3])
     own_tables.start()
     to_picks.wait()
-    for w in range(2):
+    for w in range(WAVES):
         hand_on(w, 0, inter[w])
     own_tables.wait()
     for j in range(1, MEMBERS):
@@ -356,60 +380,76 @@
     fit[0] = lines[4, 0, 0]
     loads[2].wait()
 
-    early = {(0, 2, 0): [0], (1, 2, 0): [1], (1, 2, 1): [NZ - 1], (1, 3, 0): [2], (1, 4, 0): [NZ - 2]}
-    for w in range(2):
+    early = {
+        (0, 2, 0): [(0, 0), (1, 0)],
+        (0, 3, 0): [(0, 1), (0, NZ - 1)],
+        (1, 1, 0): [(0, 2), (0, NZ - 2)],
+        (1, 2, 0): [(0, 3), (0, NZ - 3)],
+        (1, 3, 0): [(0, 4)],
+        (2, 2, 0): [(1, 1)],
+        (2, 2, 1): [(1, NZ - 1)],
+        (2, 3, 0): [(1, 2)],
+        (2, 4, 0): [(1, NZ - 2)],
+    }
+    for w in range(WAVES):
         for hop in range(1, HOPS + 1):
             pieces = len(chunk_bounds(hop))
             for k in range(pieces):
                 for way in range(2):
                     ring_copy(w, way, hop, k).wait_recv()
                 if k < pieces - 1:
-                    between = w == 0 and hop == HOPS - 1
+                    between = w < WAVES - 1 and hop == HOPS - 1
                     if between:
                         for late in range(HOPS - 1):
-                            ring_copy(1, 0, 1, late).start()
-                            ring_copy(1, 1, 1, late).start()
+                            ring_copy(w + 1, 0, 1, late).start()
+                            ring_copy(w + 1, 1, 1, late).start()
                     ring_copy(w, 0, hop + 1, k).start()
                     ring_copy(w, 1, hop + 1, k).start()
                     if between:
-                        ring_copy(1, 0, 1, HOPS - 1).start()
-                        ring_copy(1, 1, 1, HOPS - 1).start()
-                    for d in early.get((w, hop, k), ()):
-                        images(d)
+                        ring_copy(w + 1, 0, 1, HOPS - 1).start()
+                        ring_copy(w + 1, 1, 1, HOPS - 1).start()
+                    for h, d in early.get((w, hop, k), ()):
+                        images(h, d)
             hand_on(w, hop, up[w][hop])
             if hop < HOPS:
                 hand_on(w, NZ - hop, down[w][hop])
-            if k == pieces - 1:
-                for d in early.get((w, hop, k), ()):
-                    images(d)
+            for h, d in early.get((w, hop, pieces - 1), ()):
+                images(h, d)
     for d in (HOPS - 1, NZ - HOPS + 1, HOPS):
-        images(d)
+        images(1, d)
 
     def settle(d):
-        for dx in range(1, NX):
-            term_copy(d, dx).wait_recv()
-        first = ((z + NZ - d) % NZ) * per_source
+        for h in range(2):
+            for dx in range(1, NX):
+                term_copy(h, d, dx).wait_recv()
+        first = ((z + NZ - d) % NZ) * MEMBERS
 
         def add(i, carry):
-            slot = first + i
-            own[slot] += (
-                taken[0, slot].astype(jnp.float32)
-                + taken[1, slot].astype(jnp.float32)
-                + taken[2, slot].astype(jnp.float32)
+            at = first + i
+            left_half, right_half = (
+                own[h, at]
+                + (
+                    taken[h, 0, at].astype(jnp.float32)
+                    + taken[h, 1, at].astype(jnp.float32)
+                    + taken[h, 2, at].astype(jnp.float32)
+                )
+                for h in range(2)
             )
+            full[at * CAP] = jnp.where(low_rows, left_half, turned(right_half))
+            full[at * CAP + 1] = jnp.where(low_rows, turned(left_half), right_half)
             return carry
 
-        lax.fori_loop(0, per_source, add, 0, unroll=4)
+        lax.fori_loop(0, MEMBERS, add, 0, unroll=4)
 
     for d in (0, 1, NZ - 1, 2, NZ - 2, HOPS - 1, NZ - HOPS + 1, HOPS):
         settle(d)
 
     def total(p, run):
-        run = own[lines[0, 0, p]] + lines[1, 0, p].astype(jnp.float32) * run
+        run = full[lines[0, 0, p]] + lines[1, 0, p].astype(jnp.float32) * run
         runs[p] = run
         return run
 
-    lax.fori_loop(0, slots, total, jnp.zeros(own.shape[1:], jnp.float32), unroll=8)
+    lax.fori_loop(0, slots, total, jnp.zeros(full.shape[1:], jnp.float32), unroll=8)
 
     def give(l, carry):
         kept = lines[3, 0, l].astype(jnp.float32)
@@ -418,7 +458,7 @@
 
     lax.fori_loop(0, out.shape[0], give, 0, unroll=8)
 
-    for w in range(2):
+    for w in range(WAVES):
         for way in range(2):
             for hop, k in number:
                 ring_copy(w, way, hop, k).wait_send()
@@ -429,10 +469,11 @@
 
     def sent(d, carry):
         for j in range(1, MEMBERS):
-            row_copy(0, d, j).wait_send()
-            row_copy(1, d, j).wait_send()
-        for dx in range(1, NX):
-            term_copy(d, dx).wait_send()
+            for w in range(WAVES):
+                row_copy(w, d, j).wait_send()
+        for h in range(2):
+            for dx in range(1, NX):
+                term_copy(h, d, dx).wait_send()
         return carry
 
     lax.fori_loop(0, NZ, sent, 0)
@@ -492,10 +533,15 @@
     dma = pltpu.SemaphoreType.DMA
     pieces = sum(range(1, HOPS + 1))
 
-    def blocks(*lead):
-        return pltpu.VMEM((*lead, width, width), jnp.bfloat16)
-
-    wave = [blocks(REACH[h]) for h in (0, 1, 2)] * 2 + [blocks(2 * REACH[3])]
+    def blocks(*lead, tall=width):
+        return pltpu.VMEM((*lead, tall, width), jnp.bfloat16)
+
+    talls = (width, width // 2, width // 2)
+    inter = [blocks(sec_dev, tall=t) for t in talls]
+    waves = []
+    for t in talls:
+        waves += [blocks(REACH[h], tall=t) for h in (0, 1, 2)] * 2 + [blocks(2 * REACH[3], tall=t)]
+    row_blocks = [blocks(NZ, MEMBERS, tall=CAP * t) for t in talls]
     return pl.pallas_call(
         ring_kernel,
         out_shape=(
@@ -508,14 +554,13 @@
             blocks(sec_dev),
             blocks(terms, sec_dev),
             blocks(terms, sec_dev),
-            blocks(sec_dev),
-            blocks(sec_dev),
-            *wave,
-            *wave,
-            pltpu.VMEM((2, NZ, MEMBERS, CAP * width, width), jnp.bfloat16),
-            pltpu.VMEM((2, NZ, MEMBERS, CAP * width, width), jnp.bfloat16),
-            pltpu.VMEM((NX - 1, slots, rows, width), jnp.bfloat16),
-            pltpu.VMEM((NX - 1, slots, rows, width), jnp.bfloat16),
+            *inter,
+            *waves,
+            *row_blocks,
+            *row_blocks,
+            pltpu.VMEM((2, NX - 1, slots // CAP, rows, width), jnp.bfloat16),
+            pltpu.VMEM((2, NX - 1, slots // CAP, rows, width), jnp.bfloat16),
+            pltpu.VMEM((2, slots // CAP, rows, width), jnp.float32),
             pltpu.VMEM((slots, rows, width), jnp.float32),
             pltpu.VMEM((slots, rows, width), jnp.float32),
             pltpu.VMEM((1, slots), jnp.int32),
@@ -529,12 +574,12 @@
             pltpu.SMEM((5, 1, slots), jnp.int32),
             dma((3,)),
             dma((6,)),
-            dma((2, 2, pieces)),
-            dma((2, 2, pieces)),
-            dma((2, NZ, MEMBERS)),
-            dma((2, NZ, MEMBERS)),
-            dma((NZ, NX)),
-            dma((NZ, NX)),
+            dma((WAVES, 2, pieces)),
+            dma((WAVES, 2, pieces)),
+            dma((WAVES, NZ, MEMBERS)),
+            dma((WAVES, NZ, MEMBERS)),
+            dma((2, NZ, NX)),
+            dma((2, NZ, NX)),
             dma((NZ,)),
             dma((NZ,)),
             dma((MEMBERS,)),

time: 158 us -> 155 us (0.981)
  Pallas kernels: 157 us -> 153 us
    pallas_call x1, Pallas kernels: 157 us -> 153 us  [ring_exchange(): pl.pallas_call(ring_kernel, out_shape=(jax.ShapeDtypeStruct((sec_dev, row...]
where the time goes in v6:
time: 155 us
  Pallas kernels  153 us (99%)
    pallas_call x1, Pallas kernels, ring_exchange(): pl.pallas_call(ring_kernel, out_shape=(jax.ShapeDtypeStruct((sec_dev, row...  153 us

profile of v6, /device:TPU:1, one launch (start us, length us, event | category | flops | bytes accessed | tf_op | source)
XLA Modules:
  0.0 154.6 jit_solution(8730148745963505776)
XLA Ops:
  0.0 0.0 copy-start
  0.0 0.0 copy-start.1
  0.0 152.8 %ring.1 = (bf16[64,32,128]{2,1,0:T(8,128)(2,1)S(1)}, s32[1]{0:T(128)}) custom-call(s32[1,64]{1,0:T(1,128)} %bitcast.20, s32[1,64]{1,0:T(1,128)} %bitcast.18, bf16[64,128,128]{2,1,0:T(8,128)(2,1)} %psi_far.1, bf16[2,64,128,128]{3,2,1,0:T(8,128)(2,1)} %right_far.1, bf16[2,64,128,128]{3,2,1,0:T(8,128)(2,1)} %left_far.1), custom_call_target="tpu_custom_call" | custom-call | tf_op jit(solution)/shard_map/ring/pallas_call | solution.py:545
  153.5 0.0 copy-done
  153.5 0.0 copy-done.1
  153.5 0.2 conditional.1
  153.8 0.8 copy.24
Async XLA Ops:
  0.0 153.5 %copy-start = (s32[64,1]{0,1:T(1,128)S(1)}, s32[64,1]{0,1:T(1,128)}, u32[]{:S(2)}) copy-start(s32[64,1]{0,1:T(1,128)} %param.11) | copy-start | bytes 772
  0.0 153.5 %copy-start.1 = (s32[64,1]{0,1:T(1,128)S(1)}, s32[64,1]{0,1:T(1,128)}, u32[]{:S(2)}) copy-start(s32[64,1]{0,1:T(1,128)} %param.10) | copy-start | bytes 772

commit v7 on v6

--- a/solution.py
+++ b/solution.py
@@ -389,7 +389,7 @@
         (2, 2, 0): [(1, 1)],
         (2, 2, 1): [(1, NZ - 1)],
         (2, 3, 0): [(1, 2)],
-        (2, 4, 0): [(1, NZ - 2)],
+        (2, 3, 1): [(1, NZ - 2)],
     }
     for w in range(WAVES):
         for hop in range(1, HOPS + 1):

time: 155 us -> 155 us (level)
  no operation moved by 1% of the time
where the time goes in v7:
time: 155 us
  Pallas kernels  153 us (99%)
    pallas_call x1, Pallas kernels, ring_exchange(): pl.pallas_call(ring_kernel, out_shape=(jax.ShapeDtypeStruct((sec_dev, row...  153 us

profile of v7, /device:TPU:1, one launch (start us, length us, event | category | flops | bytes accessed | tf_op | source)
XLA Modules:
  0.0 154.6 jit_solution(18003011181872246602)
XLA Ops:
  0.0 0.0 copy-start
  0.0 0.0 copy-start.1
  0.0 152.8 %ring.1 = (bf16[64,32,128]{2,1,0:T(8,128)(2,1)S(1)}, s32[1]{0:T(128)}) custom-call(s32[1,64]{1,0:T(1,128)} %bitcast.20, s32[1,64]{1,0:T(1,128)} %bitcast.18, bf16[64,128,128]{2,1,0:T(8,128)(2,1)} %psi_far.1, bf16[2,64,128,128]{3,2,1,0:T(8,128)(2,1)} %right_far.1, bf16[2,64,128,128]{3,2,1,0:T(8,128)(2,1)} %left_far.1), custom_call_target="tpu_custom_call" | custom-call | tf_op jit(solution)/shard_map/ring/pallas_call | solution.py:545
  153.5 0.0 copy-done
  153.5 0.0 copy-done.1
  153.5 0.2 conditional.1
  153.8 0.8 copy.24
Async XLA Ops:
  0.0 153.5 %copy-start = (s32[64,1]{0,1:T(1,128)S(1)}, s32[64,1]{0,1:T(1,128)}, u32[]{:S(2)}) copy-start(s32[64,1]{0,1:T(1,128)} %param.11) | copy-start | bytes 772
  0.0 153.5 %copy-start.1 = (s32[64,1]{0,1:T(1,128)S(1)}, s32[64,1]{0,1:T(1,128)}, u32[]{:S(2)}) copy-start(s32[64,1]{0,1:T(1,128)} %param.10) | copy-start | bytes 772
